TPU v7x, 32 devices: a whole 2x2x4 slice. The times are simulated.
32 devices in a mesh: dp: 4 (over z), fsdp: 8 (over y, x, core).
Axes of the slice: x: 2, y: 2, z: 4, core: 2. Of those that a mesh axis runs over, the one named last changes fastest.
Arguments:
- block_input: bfloat16 [2, 32, 576, 768], P(None, ('dp', 'fsdp')), may hold values from -6 to 6
- valid_counts: int32 [2, 32], P(None, ('dp', 'fsdp')), may hold values from 288 to 576
- output_cotangent: bfloat16 [2, 32, 576, 768], P(None, ('dp', 'fsdp')), may hold values from -6 to 6
- triple_weight: float32 [768, 2304], P(('dp', 'fsdp')), may hold values from -0.21875 to 0.21875
- merge_weight: float32 [768, 768], P(('dp', 'fsdp')), may hold values from -0.875 to 0.875
- expand_weight: float32 [768, 3072], P(('dp', 'fsdp')), may hold values from -0.21875 to 0.21875
- reduce_weight: float32 [3072, 768], P(('dp', 'fsdp')), may hold values from -0.109375 to 0.109375
- first_gain: float32 [768], P(('dp', 'fsdp')), may hold values from 0.25 to 1.75
- first_shift: float32 [768], P(('dp', 'fsdp')), may hold values from -3 to 3
- query_bias: float32 [768], P(('dp', 'fsdp')), may hold values from -3 to 3
- value_bias: float32 [768], P(('dp', 'fsdp')), may hold values from -3 to 3
- merge_bias: float32 [768], P(('dp', 'fsdp')), may hold values from -3 to 3
- second_gain: float32 [768], P(('dp', 'fsdp')), may hold values from 0.25 to 1.75
- second_shift: float32 [768], P(('dp', 'fsdp')), may hold values from -3 to 3
- expand_bias: float32 [3072], P(('dp', 'fsdp')), may hold values from -3 to 3
- reduce_bias: float32 [768], P(('dp', 'fsdp')), may hold values from -3 to 3
- position_table: float32 [529, 24], replicated, may hold values from -4 to 4
Outputs:
- block_output: bfloat16 [2, 32, 576, 768], P(None, ('dp', 'fsdp'))
- input_grad: bfloat16 [2, 32, 576, 768], P(None, ('dp', 'fsdp'))
- triple_grad: float32 [768, 2304], P(('dp', 'fsdp'))
- merge_grad: float32 [768, 768], P(('dp', 'fsdp'))
- expand_grad: float32 [768, 3072], P(('dp', 'fsdp'))
- reduce_grad: float32 [3072, 768], P(('dp', 'fsdp'))
- first_gain_grad: float32 [768], P(('dp', 'fsdp'))
- first_shift_grad: float32 [768], P(('dp', 'fsdp'))
- query_bias_grad: float32 [768], P(('dp', 'fsdp'))
- value_bias_grad: float32 [768], P(('dp', 'fsdp'))
- merge_bias_grad: float32 [768], P(('dp', 'fsdp'))
- second_gain_grad: float32 [768], P(('dp', 'fsdp'))
- second_shift_grad: float32 [768], P(('dp', 'fsdp'))
- expand_bias_grad: float32 [3072], P(('dp', 'fsdp'))
- reduce_bias_grad: float32 [768], P(('dp', 'fsdp'))
- position_table_grad: float32 [529, 24], replicated
Inputs may be any that keep to these rules, and one draw needn't show every extreme that they name: `valid_counts`: tokens at raster positions from the count on are padding: they are no keys, and their attention output is zero.
All inputs are finite; a program needn't handle non-finite values.
Results may differ from a plain program's by a relative error of at most 0.012.
The roundings to bfloat16 on the way count: a program that leaves them out, or rounds other values in their place, can miss the bound.
Values may be sent and summed in bfloat16 or wider, within the bound.
A program may use at most 192 MiB of HBM per device.

v0:
```python
import math
import functools

import numpy as np
import jax
import jax.numpy as jnp
from jax import lax
from jax.experimental import pallas as pl
from jax.experimental.pallas import tpu as pltpu
from jax.sharding import PartitionSpec as P

D = 768
FF = 3072
HEADS = 24
HEAD_DIM = 32
WIN = 12
SIDE = 24
SHIFT = 6
TOK = SIDE * SIDE
ROWS = 2 * TOK
WT = WIN * WIN
EXT = 2 * WIN - 1
GROUPS = 3
GH = HEADS // GROUPS
GW = GH * HEAD_DIM
QL = GH * WT
SCALE = HEAD_DIM ** -0.5
MASKED = -1e30
EPS = 1e-5
F32 = jnp.float32
BF16 = jnp.bfloat16
VMEM_LIMIT = 63 << 20
AXES = ("dp", "fsdp")
MESH = pl.DeviceIdType.MESH
ANY = pl.BlockSpec(memory_space=pl.ANY)
VM = pl.BlockSpec(memory_space=pltpu.VMEM)
SM = pl.BlockSpec(memory_space=pltpu.SMEM)
every = slice(None)

NN = (((1,), (0,)), ((), ()))
NT = (((1,), (1,)), ((), ()))
TN = (((0,), (0,)), ((), ()))


def dot(a, b, dims=NN):
    return lax.dot_general(a, b, dims, preferred_element_type=F32)


def layout_constants():
    j = np.arange(WT)
    reg = lambda c: (c >= SIDE - WIN).astype(np.int32) + (c >= SIDE - SHIFT).astype(np.int32)
    raster, label = np.zeros((4, WT), np.int32), np.zeros((4, WT), np.int32)
    for w in range(4):
        rr = (w // 2) * WIN + j // WIN
        rc = (w % 2) * WIN + j % WIN
        raster[w] = ((rr + SHIFT) % SIDE) * SIDE + (rc + SHIFT) % SIDE
        label[w] = reg(rr) * 3 + reg(rc)
    target = np.full((4, WT), -1, np.int32)
    for p in range(4):
        r = j // WIN + (WIN - 1 if p // 2 == 0 else -1)
        s = j % WIN + (WIN - 1 if p % 2 == 0 else -1)
        target[p] = np.where((r >= 0) & (s >= 0), r * EXT + s, -1)
    spread = lambda v: np.broadcast_to(v.reshape(1, TOK), (8, TOK)).astype(np.int32)
    return np.broadcast_to(np.tile(label, (1, GH))[:, None, :], (4, 8, QL)).astype(np.int32), spread(target), spread(raster)


LABEL_Q, TARGET, RASTER_Q = layout_constants()


def fill_places(raster, label=None):
    j = lax.broadcasted_iota(jnp.int32, (WT, 128), 0)
    a = (j * 171) >> 11
    c = j - a * WIN
    reg = lambda v: (v >= SIDE - WIN).astype(jnp.int32) + (v >= SIDE - SHIFT).astype(jnp.int32)
    turn = lambda v: jnp.where(v >= SIDE - SHIFT, v + SHIFT - SIDE, v + SHIFT)
    for w in range(4):
        rr, rc = a + (w // 2) * WIN, c + (w % 2) * WIN
        raster[w] = turn(rr) * SIDE + turn(rc)
        if label is not None:
            label[w] = reg(rr) * 3 + reg(rc)


def lane_iota(shape):
    return lax.broadcasted_iota(jnp.int32, shape, len(shape) - 1)


def aligned(v, n):
    return v if isinstance(v, int) else pl.multiple_of(v, n)


def lanes(start, width):
    return pl.ds(aligned(start, 128), width)


def window(i):
    return pl.ds(aligned(i * WT, WT), WT)


def to_window(raster, w):
    return (raster[w][:, 0:1] == lane_iota((WT, TOK))).astype(BF16)


def to_raster(raster_q, m):
    t = lax.broadcasted_iota(jnp.int32, (WT, TOK), 0) + m * WT
    return (raster_q[0:1, :] == t).astype(BF16)


def stats(x):
    mean = jnp.mean(x, axis=-1, keepdims=True)
    center = x - mean
    var = jnp.mean(center * center, axis=-1, keepdims=True)
    inv = lax.rsqrt(var + EPS)
    return center * inv, inv


def head_stack(dst, x):
    lane = lane_iota(x.shape) // HEAD_DIM
    zero = jnp.zeros_like(x)
    for h in range(GH):
        dst[h * WT:(h + 1) * WT, :] = jnp.where(lane == h, x, zero)


def head_pick(o):
    lane = lane_iota((WT, GW)) // HEAD_DIM
    out = jnp.where(lane == 0, o[0:WT], 0.0)
    for h in range(1, GH):
        out = jnp.where(lane == h, o[h * WT:(h + 1) * WT], out)
    return out


def onehot(target_ref):
    t = lax.broadcasted_iota(jnp.int32, (EXT * EXT, 4 * WT), 0)
    return (t == target_ref[0:1, :]).astype(F32)


def table_rows(table_ref, target_ref, t4):
    t4[...] = lax.dot_general(table_ref[...], onehot(target_ref), NN,
                              precision=lax.Precision.HIGHEST, preferred_element_type=F32) * (1.0 / SCALE)


def spread_bias(g, t4, bias, rowbuf):
    a_of = (lane_iota((1, QL)) % WT) // WIN
    c_of = lane_iota((16, QL)) % WIN
    rows = []
    for p in range(4):
        acc = jnp.zeros((1, QL), F32)
        for h in range(GH):
            piece = t4[pl.ds(g * GH + h, 1), p * WT:(p + 1) * WT]
            piece = jnp.concatenate([piece, jnp.zeros((1, QL - WT), F32)], axis=1)
            acc = acc + (pltpu.roll(piece, h * WT, axis=1) if h else piece)
        rows.append(acc)
    for s in range(2):
        for b in range(WIN):
            pos = pltpu.roll(rows[s], WIN * b, axis=1) if b else rows[s]
            neg = pltpu.roll(rows[2 + s], (WIN * b - WT) % QL, axis=1)
            rowbuf[s, b:b + 1, :] = jnp.where(a_of >= b, pos, neg)
    for d in range(WIN):
        pos = pltpu.roll(rowbuf[0], d, axis=1) if d else rowbuf[0]
        neg = pltpu.roll(rowbuf[1], (d - WIN) % QL, axis=1)
        both = jnp.where(c_of >= d, pos, neg)
        for n in range(9):
            bias[g * 9 + n, pl.ds(d, WIN, stride=WIN), :] = both[0:WIN, n * 128:(n + 1) * 128]


def gather_bias(g, bgrad, accbuf, t4):
    a_of = (lane_iota((1, QL)) % WT) // WIN
    c_of = lane_iota((WIN, QL)) % WIN
    pos = jnp.zeros((WIN, QL), F32)
    neg = jnp.zeros((WIN, QL), F32)
    for d in range(WIN):
        r = jnp.concatenate([bgrad[n, pl.ds(d, WIN, stride=WIN), :] for n in range(9)], axis=1)
        p = jnp.where(c_of >= d, r, 0.0)
        pos = pos + (pltpu.roll(p, QL - d, axis=1) if d else p)
        if d:
            neg = neg + pltpu.roll(jnp.where(c_of < d, r, 0.0), WIN - d, axis=1)
    accbuf[0, 0:WIN, :] = pos
    accbuf[1, 0:WIN, :] = neg
    for s in range(2):
        pp = jnp.zeros((1, QL), F32)
        nn = jnp.zeros((1, QL), F32)
        for b in range(WIN):
            r = accbuf[s, b:b + 1, :]
            p = jnp.where(a_of >= b, r, 0.0)
            pp = pp + (pltpu.roll(p, QL - WIN * b, axis=1) if b else p)
            if b:
                nn = nn + pltpu.roll(jnp.where(a_of < b, r, 0.0), WT - WIN * b, axis=1)
        for part, row in ((s, pp), (2 + s, nn)):
            for h in range(GH):
                moved = pltpu.roll(row, QL - h * WT, axis=1) if h else row
                t4[pl.ds(g * GH + h, 1), part * WT:(part + 1) * WT] = moved[:, 0:WT]


ERF_SLOPE = 0.35
ERF_FIT = (0.19434814435164116, 0.235843067071591, -0.008625688056468914, 0.6849613674275746, -0.6811631064960405, 0.7727015621272543, -0.19806535099226122)


def gelu_pair(v):
    e = jnp.exp(v * v * -0.5)
    t = 1.0 / (1.0 + jnp.abs(v) * (ERF_SLOPE * math.sqrt(0.5)))
    poly = jnp.full_like(t, 0.5 * ERF_FIT[-1])
    for c in ERF_FIT[-2::-1]:
        poly = poly * t + 0.5 * c
    tail = poly * t * e
    cdf = jnp.where(v >= 0, 1.0 - tail, tail)
    return v * cdf, cdf + v * e * (1.0 / math.sqrt(2.0 * math.pi))


def norm_back(hat, inv, gain, grad):
    scaled = grad * gain
    return inv * (scaled - jnp.mean(scaled, axis=-1, keepdims=True)
                  - hat * jnp.mean(scaled * hat, axis=-1, keepdims=True))


class Place:
    def __init__(self, dims):
        self.nz, self.ny, self.nx = dims
        f = lax.axis_index("fsdp")
        self.z = lax.axis_index("dp")
        self.c = lax.rem(f, 2)
        self.x = lax.rem(f // 2, self.nx)
        self.y = f // (2 * self.nx)

    def size(self, axis):
        return {"z": self.nz, "y": self.ny, "x": self.nx, "c": 2}[axis]

    def at(self, axis):
        return {"z": self.z, "y": self.y, "x": self.x, "c": self.c}[axis]

    def step(self, axis, k):
        return lax.rem(self.at(axis) + k, self.size(axis))

    def back(self, axis, k):
        return self.step(axis, self.size(axis) - k)

    def device(self, axis, k):
        p = {a: (self.step(a, k) if a == axis else self.at(a)) for a in "zyxc"}
        return (p["z"], (p["y"] * self.nx + p["x"]) * 2 + p["c"])

    def greet(self):
        barrier = pltpu.get_barrier_semaphore()
        total = 0
        for axis in "czyx":
            for k in range(1, self.size(axis)):
                pl.semaphore_signal(barrier, inc=1, device_id=self.device(axis, k), device_id_type=MESH)
                total += 1
        pl.semaphore_wait(barrier, total)


def mesh_dims(mesh):
    chips = mesh.shape["fsdp"] // 2
    ny = max(n for n in range(1, chips + 1) if n * n <= chips and chips % n == 0)
    return mesh.shape["dp"], ny, chips // ny


class Swap:
    def __init__(self, place, axis, sems, src, dst, came, has=None):
        self.has = has
        self.place, self.axis, self.sems = place, axis, sems
        self.src, self.dst, self.came = src, dst, came

    def make(self, k, src, dst):
        return pltpu.make_async_remote_copy(
            src_ref=src(k), dst_ref=dst(k), send_sem=self.sems[0](k), recv_sem=self.sems[1](k),
            device_id=self.place.device(self.axis, k), device_id_type=MESH)

    def peers(self):
        return range(1, self.place.size(self.axis))

    def each(self, sender, act):
        for k in self.peers():
            if self.has is None:
                act(k)
            else:
                pl.when(self.has(sender(k)))(lambda k=k: act(k))

    def start(self):
        self.each(lambda k: self.place.at(self.axis), lambda k: self.make(k, self.src, self.dst).start())

    def arrive(self):
        self.each(lambda k: self.place.back(self.axis, k), lambda k: self.make(k, self.came, self.came).wait_recv())

    def done(self):
        self.each(lambda k: self.place.at(self.axis), lambda k: self.make(k, self.src, self.dst).wait_send())


def when(cond, body):
    if isinstance(cond, (bool, np.bool_)):
        if cond:
            body()
    else:
        pl.when(cond)(body)


def both(*conds):
    out = True
    for c in conds:
        if isinstance(c, (bool, np.bool_)):
            if not c:
                return False
        else:
            out = c if out is True else jnp.logical_and(out, c)
    return out


def call(kernel, outs, scratch, ins, name):
    return pl.pallas_call(
        kernel, out_shape=[jax.ShapeDtypeStruct(s, d) for s, d in outs], in_specs=[VM] * len(ins),
        out_specs=[VM] * len(outs), scratch_shapes=scratch, name=name,
        compiler_params=pltpu.CompilerParams(vmem_limit_bytes=VMEM_LIMIT))(*ins)


HALF = 4 * D
TM_HALF = 2 * D
FF_HALF = FF // 2
FF_PART = FF // 4


class Gather:
    def __init__(self, place, w, half, base, n_w, r, part, send, recv):
        self.place = place
        self.w, self.half, self.base, self.n_w, self.r, self.part = w, half, base, n_w, r, part
        self.send, self.recv = send, recv
        self.n = n_w + 3

    def block(self, wide, p, c):
        if wide:
            return (every, lanes(c * self.half + self.base + p * 256, 256))
        return (every, lanes(c * (D // 2) + p * 128, 128))

    def swap(self, wide, p, odd, s):
        pc = self.place
        ref = self.w if wide else self.r
        q = p if wide else self.n_w + p
        sems = (lambda k: self.send.at[q, s, k - 1], lambda k: self.recv.at[q, s, k - 1])
        blk = self.block(wide, p, pc.c)
        zs = every if wide else pl.ds(self.part * (pc.nz // 2), pc.nz // 2)
        at = lambda zz, yy, xx, b=blk: ref.at[(zz, yy, xx) + b]
        z, y, x = pc.z, pc.y, pc.x
        if s == 0:
            has = None if wide else (lambda zz: (zz >= pc.nz // 2) == (self.part == 1))
            own = lambda k: at(z, y, x)
            return Swap(pc, "z", sems, own, own, lambda k: at(pc.back("z", k), y, x), has)
        if s == 3:
            mine = lambda k: at(zs, every, every)
            return Swap(pc, "c", sems, mine, mine, lambda k: at(zs, every, every, self.block(wide, p, 1 - pc.c)))
        first = "y" if odd else "x"
        if s == 1:
            own = lambda k: at(zs, y, x)
            if first == "x":
                return Swap(pc, "x", sems, own, own, lambda k: at(zs, y, pc.back("x", k)))
            return Swap(pc, "y", sems, own, own, lambda k: at(zs, pc.back("y", k), x))
        if first == "x":
            own = lambda k: at(zs, y, every)
            return Swap(pc, "y", sems, own, own, lambda k: at(zs, pc.back("y", k), every))
        own = lambda k: at(zs, every, x)
        return Swap(pc, "x", sems, own, own, lambda k: at(zs, every, pc.back("x", k)))

    def on_piece(self, p, body):
        when(both(p >= 0, p < self.n_w), lambda: body(True, p))
        when(both(p >= self.n_w, p < self.n), lambda: body(False, p - self.n_w))

    def tick(self, u, odd, landed=None):
        def last(wide, p):
            self.swap(wide, p, odd, 3).arrive()
            if landed is not None:
                landed(wide, p)

        def step(s):
            def body(wide, p):
                if s:
                    self.swap(wide, p, odd, s - 1).arrive()
                self.swap(wide, p, odd, s).start()
            return body

        self.on_piece(u - 8, last)
        for s in (3, 2, 1, 0):
            self.on_piece(u - 2 * s, step(s))

    def finish(self):
        for q in range(self.n):
            for s in range(4):
                self.swap(q < self.n_w, q if q < self.n_w else q - self.n_w, q % 2 == 1, s).done()


def small_swap(pc, sb, send, recv, s):
    sems = (lambda k: send.at[s, k - 1], lambda k: recv.at[s, k - 1])
    at = lambda zz, yy, xx, c=pc.c: sb.at[zz, yy, xx, c]
    z, y, x = pc.z, pc.y, pc.x
    own = [lambda k: at(z, y, x), lambda k: at(every, y, x), lambda k: at(every, y, every),
           lambda k: at(every, every, every)][s]
    came = [lambda k: at(pc.back("z", k), y, x), lambda k: at(every, y, pc.back("x", k)),
            lambda k: at(every, pc.back("y", k), every), lambda k: at(every, every, every, 1 - pc.c)][s]
    return Swap(pc, "zxyc"[s], sems, own, own, came)


def place_small(sb, sv, eb, n_small, n_wide):
    nz, ny, nx = sb.shape[:3]
    for out, row0, width, total in ((sv, 0, n_small, D), (eb, 8, n_wide, FF)):
        tiles = [jnp.zeros((8, 128), F32) for _ in range(total // 128)]
        lane = lane_iota((8, 128))
        n = 0
        for q in range(nz * ny * nx):
            for c in range(2):
                blk = sb[q // (ny * nx), (q // nx) % ny, q % nx, c, row0:row0 + 8, :]
                tile, off = divmod(n * width, 128)
                moved = pltpu.roll(blk, off, axis=1) if off else blk
                end = off + width
                tiles[tile] = jnp.where((lane >= off) & (lane < min(end, 128)), moved, tiles[tile])
                if end > 128:
                    tiles[tile + 1] = jnp.where(lane < end - 128, moved, tiles[tile + 1])
                n += 1
        out[...] = jnp.concatenate(tiles, axis=1)


def group_cols(g):
    return (((0, g * 384, 256),), ((0, g * 384 + 256, 128), (1, g * 384, 128)), ((1, g * 384 + 128, 256),))


def merge_cols(n):
    return tuple((b // 3, 1152 + lax.rem(b, 3) * 128, 128) for b in (2 * n, 2 * n + 1))


def columns(ref, parts, half):
    take = [ref[:, lanes(h * half + lo, n)] for h, lo, n in parts]
    return take[0] if len(take) == 1 else jnp.concatenate(take, axis=1)


class Flat:
    def __init__(self, ref):
        self.ref = ref

    def __getitem__(self, idx):
        v = self.ref[:, :, :, :, idx[1]]
        return v.reshape(-1, v.shape[-1])


def own_halves(h):
    for g in range(GROUPS):
        yield 0, g * GW + h * 2 * D, g * 384 + h * 128, 256
        yield 0, D + g * GW + h * 128, g * 384 + 256 * (1 - h), 128
    yield 1, h * (D // 2), 1152, D // 2
    for s in range(2):
        yield 2, s * FF_HALF + h * FF_PART, TM_HALF + s * FF_PART, FF_PART
    yield 3, h * (D // 2), 0, D // 2


def forward_kernel(near, dims, counts, x, labq, target, table, *rest):
    n_in = 13 if near else 4
    given = rest[:n_in]
    (o_w, o_r, o_triple, o_pt, o_att, o_mixed, o_n2, o_normed, o_xp, sv, eb, o_ew, o_er,
     w, r, sb, stage_w, stage_r, xp, normed, triple, attended, mixed, n2, pt, t4, bias, rowbuf, qs, st, lk, raster, labk,
     send, recv, ssend, srecv, lsem, psem) = rest[n_in:]

    def keep(n, src, dst):
        return pltpu.make_async_copy(src, dst, lsem.at[n])

    if near:
        pc = Place(dims)
        gather = Gather(pc, w, HALF, 0, 9, r, 0, send, recv)

    def part_of(wide, p):
        zs = every if wide else pl.ds(0, dims[0] // 2)
        for c in range(2):
            n = 2 * (p if wide else 9 + p) + c
            blk = (zs, every, every) + gather.block(wide, p, c)
            yield (keep(n, w.at[blk], o_w.at[blk]) if wide else keep(n, r.at[blk], o_r.at[blk]))

    def landed(wide, p):
        for copy in part_of(wide, p):
            copy.start()

    def small_tick(u):
        if u:
            small_swap(pc, sb, ssend, srecv, u // 2 - 1).arrive()
        if u < 8:
            small_swap(pc, sb, ssend, srecv, u // 2).start()

    if near:
        pc.greet()
        own, vectors = given[:4], given[4:]
        first = []
        for i, ((n, src, dst, width), (_, _, back, _)) in enumerate(zip(own_halves(1 - pc.c), own_halves(pc.c))):
            ref, stage = own[n], (stage_r if n == 3 else stage_w)
            rows = lambda c, m=ref.shape[0]: pl.ds(aligned(c * m, 8), m)
            sems = (lambda k, i=i: ssend.at[4 + i, 0], lambda k, i=i: srecv.at[4 + i, 0])
            first.append(Swap(pc, "c", sems, lambda k, v=ref.at[:, lanes(src, width)]: v,
                              lambda k, v=stage.at[rows(pc.c), lanes(dst, width)]: v,
                              lambda k, v=stage.at[rows(1 - pc.c), lanes(back, width)]: v))
        for s in first:
            s.start()
        sb[pc.z, pc.y, pc.x, pc.c] = jnp.zeros((16, 128), F32)
        for k, v in enumerate(vectors):
            sb[pc.z, pc.y, pc.x, pc.c, k, 0:v.shape[0]] = v[...].astype(BF16).astype(F32)
        for n, src, dst, width in own_halves(pc.c):
            ref, stage = own[n], (stage_r if n == 3 else stage_w)
            stage[pl.ds(aligned(pc.c * ref.shape[0], 8), ref.shape[0]), lanes(dst, width)] = ref[:, lanes(src, width)]
        for s in first[:-1]:
            s.arrive()
        w[pc.z, pc.y, pc.x, :, lanes(pc.c * HALF, HALF)] = stage_w[...].astype(BF16)
        gather.tick(0, False)
        small_tick(0)
        gather.tick(1, True)
        first[-1].arrive()
        r[pc.z, pc.y, pc.x, :, lanes(pc.c * (D // 2), D // 2)] = stage_r[...].astype(BF16)
        o_ew[...] = stage_w[:, TM_HALF + FF_PART:HALF].astype(BF16)
        o_er[...] = stage_r[...].astype(BF16)
    else:
        wown, rown, sv_in, eb_in = given
        loads = [keep(0, wown, w), keep(1, rown, r)]
        for c in loads:
            c.start()
        for c in loads:
            c.wait()
        sv[...] = sv_in[...]
        eb[...] = eb_in[...]

    def permute(i, _):
        xp[window(i), :] = dot(to_window(raster, i % 4), x[i // 4]).astype(BF16)
        return 0

    fill_places(raster, labk)
    table_rows(table, target, t4)

    def prologue(u, _):
        if near:
            for odd in range(2):
                pl.when(u % 2 == odd)(lambda odd=odd: gather.tick(u, odd == 1, landed))
            for k in range(1, 5):
                pl.when(u == 2 * k)(lambda k=k: small_tick(2 * k))

        @pl.when(u < 5)
        def _():
            spread_bias(u - 2, t4, bias, rowbuf)

        @pl.when(jnp.logical_and(u >= 5, u < 9))
        def _():
            lax.fori_loop(2 * (u - 5), 2 * (u - 4), permute, 0)

        return 0

    lax.fori_loop(2, 10, prologue, 0)
    if near:
        place_small(sb, sv, eb, given[0].shape[0], given[3].shape[0])

    def ln1(i, _):
        hat, _i = stats(xp[window(i), :].astype(F32))
        normed[window(i), :] = (hat * sv[0:1, :] + sv[1:2, :]).astype(BF16)
        return 0

    lax.fori_loop(0, 8, ln1, 0)
    keep(24, xp, o_xp).start()
    keep(25, normed, o_normed).start()
    wf = Flat(w)

    def attn(t, i, g):
        b, v = i // 4, i % 4
        rows = window(i)
        col = lambda k: lanes(g * D + k * GW, GW)
        valid = raster[v] < counts[b]
        lk[...] = jnp.where(valid, labk[v], -1)
        head_stack(qs, triple[rows, col(0)])
        st[...] = dot(triple[rows, col(1)], qs[...], NT)
        slot = t % 2
        for n in range(9):
            c = lanes(n * 128, 128)
            s = st[:, c] + bias[g * 9 + n]
            s = jnp.where(lk[...] == labq[v, 0:1, c], s, MASKED)
            m = jnp.max(s, axis=0, keepdims=True)
            e = jnp.exp((s - m) * SCALE)
            tot = jnp.sum(e, axis=0, keepdims=True)
            pt[slot, :, c] = (e * (1.0 / tot)).astype(BF16)
        pltpu.make_async_copy(pt.at[slot], o_pt.at[g * 8 + i], psem.at[slot]).start()
        out = head_pick(dot(pt[slot], triple[rows, col(2)], TN))
        vq = jnp.concatenate([valid, valid], axis=1)
        attended[rows, lanes(g * GW, GW)] = jnp.where(vq, out, 0.0).astype(BF16)

    def quarter(q, _):
        g = q // 4

        @pl.when(q % 4 == 0)
        def _():
            for k, parts in enumerate(group_cols(g)):
                v = dot(normed[...], columns(wf, parts, HALF))
                if k != 1:
                    v = v + sv[2 + k // 2:3 + k // 2, lanes(g * GW, GW)]
                triple[:, lanes(g * D + k * GW, GW)] = v.astype(BF16)

        def one(j, _):
            step = q * 2 + j

            @pl.when(step >= 2)
            def _():
                pltpu.make_async_copy(pt.at[step % 2], o_pt.at[0], psem.at[step % 2]).wait()

            attn(step, step % 8, g)
            return 0

        lax.fori_loop(0, 2, one, 0)
        if near:
            for odd in range(2):
                pl.when(q % 2 == odd)(lambda odd=odd: gather.tick(10 + q, odd == 1, landed))
        return 0

    lax.fori_loop(0, 4 * GROUPS, quarter, 0)
    keep(26, triple, o_triple).start()
    keep(27, attended, o_att).start()
    def merge(n, _):
        cols = lanes(n * 256, 256)
        v = dot(attended[...], columns(wf, merge_cols(n), HALF))
        mixed[:, cols] = xp[:, cols].astype(F32) + v + sv[4:5, cols]
        return 0

    lax.fori_loop(0, 3, merge, 0)
    keep(28, mixed, o_mixed).start()

    def ln2(i, _):
        hat, _i = stats(mixed[window(i), :])
        n2[window(i), :] = (hat * sv[5:6, :] + sv[6:7, :]).astype(BF16)
        return 0

    lax.fori_loop(0, 8, ln2, 0)
    keep(29, n2, o_n2).start()
    if near:
        gather.finish()
        for s in first:
            s.done()
        for s in range(4):
            small_swap(pc, sb, ssend, srecv, s).done()
        for q in range(12):
            for copy in part_of(q < 9, q if q < 9 else q - 9):
                copy.wait()
    for n, src, dst in ((24, xp, o_xp), (25, normed, o_normed), (26, triple, o_triple), (27, attended, o_att),
                        (28, mixed, o_mixed), (29, n2, o_n2)):
        keep(n, src, dst).wait()
    for slot in range(2):
        pltpu.make_async_copy(pt.at[slot], o_pt.at[0], psem.at[slot]).wait()


def forward(near, dims, counts, x, table, *given):
    nz, ny, nx = dims if near else (1, 1, 1)
    rw, rr = (given[0].shape[0] * 2, given[3].shape[0] * 2) if near else (D, FF)
    peers = max(nz, ny, nx, 2) - 1
    full_w, full_r = (nz, ny, nx, rw, 2 * HALF), (nz, ny, nx, rr, D)
    tiny = (8, 128)
    outs = [(full_w if near else tiny, BF16), (full_r if near else tiny, BF16), ((ROWS, 3 * D), BF16),
            ((8 * GROUPS, WT, QL), BF16), ((ROWS, D), BF16), ((ROWS, D), F32), ((ROWS, D), BF16), ((ROWS, D), BF16),
            ((ROWS, D), BF16), ((8, D), F32), ((8, FF), F32), ((rw, FF_PART) if near else tiny, BF16),
            ((rr, D // 2) if near else tiny, BF16)]
    if not near:
        given = (given[0].reshape(full_w), given[1].reshape(full_r)) + given[2:]
    vm = pltpu.VMEM
    dma = pltpu.SemaphoreType.DMA
    scratch = [vm(full_w, BF16), vm(full_r, BF16), vm((nz, ny, nx, 2, 16, 128), F32), vm((rw if near else 8, HALF), F32),
               vm((rr if near else 8, D // 2), F32), vm((ROWS, D), BF16), vm((ROWS, D), BF16), vm((ROWS, 3 * D), BF16),
               vm((ROWS, D), BF16), vm((ROWS, D), F32), vm((ROWS, D), BF16), vm((2, WT, QL), BF16),
               vm((HEADS, 4 * WT), F32), vm((GROUPS * 9, WT, 128), F32), vm((2, 16, QL), F32), vm((QL, GW), BF16),
               vm((WT, QL), F32), vm((WT, 128), jnp.int32), vm((4, WT, 128), jnp.int32), vm((4, WT, 128), jnp.int32),
               dma((12, 4, peers)), dma((12, 4, peers)), dma((14, peers)), dma((14, peers)), dma((30,)), dma((2,))]
    params = dict(collective_id=0, has_side_effects=True) if near else {}
    return pl.pallas_call(
        functools.partial(forward_kernel, near, dims),
        out_shape=[jax.ShapeDtypeStruct(s, d) for s, d in outs],
        in_specs=[SM] + [VM] * 4 + ([VM] * 13 if near else [ANY, ANY, VM, VM]),
        out_specs=[ANY] * 9 + [VM] * 4,
        scratch_shapes=scratch, name="forward",
        compiler_params=pltpu.CompilerParams(vmem_limit_bytes=VMEM_LIMIT, **params),
    )(counts, x, jnp.asarray(LABEL_Q), jnp.asarray(TARGET), table.T,
      *given)


class Scatter:
    def __init__(self, place, bufs, send, recv):
        self.place = place
        self.bufs, self.send, self.recv = bufs, send, recv

    def src(self, kind, g, i, ab, c):
        if kind == "r":
            n = g.shape[3] // 2
            return g.at[every, every, every, pl.ds(ab * n, n), lanes(c * (D // 2) + i * 128, 128)]
        return g.at[every, every, every, every, lanes(c * FF_HALF + i * 256 + ab * 128, 128)]

    def swap(self, kind, g, out, i, ab, s):
        pc = self.place
        r0, r1, r2, r3, fin = self.bufs[kind]
        q = {"e": 0, "t": 6, "r": 12}[kind] + i
        sems = (lambda k: self.send.at[q, ab, s, k - 1], lambda k: self.recv.at[q, ab, s, k - 1])
        first, second = ("y", "x") if ab == 0 else ("x", "y")
        if s == 0:
            to = lambda k: r0.at[i, ab]
            return Swap(pc, "c", sems, lambda k: self.src(kind, g, i, ab, 1 - pc.c), to, to)
        if s == 1:
            to = lambda k: r1.at[i, ab, k - 1]
            at = lambda k: (every, pc.step("y", k), every) if first == "y" else (every, every, pc.step("x", k))
            return Swap(pc, first, sems, lambda k: r0.at[(i, ab) + at(k)], to, to)
        if s == 2:
            to = lambda k: r2.at[i, ab, k - 1]
            return Swap(pc, second, sems, lambda k: r1.at[i, ab, 0, every, pc.step(second, k)], to, to)
        if s == 3:
            to = lambda k: r3.at[i, ab, k - 1]
            return Swap(pc, "z", sems, lambda k: r2.at[i, ab, 0, pc.step("z", k)], to, to)
        n = out.shape[0]
        if kind == "r":
            cols = lambda c: lanes(c * (D // 2) + i * 128, 128)
            return Swap(pc, "c", sems, lambda k: fin.at[i, 1 - pc.c], lambda k: out.at[:, cols(pc.c)],
                        lambda k: out.at[:, cols(1 - pc.c)])
        cols = lambda c: lanes(c * FF_HALF + i * 256 + ab * 128, 128)
        return Swap(pc, "c", sems, lambda k: fin.at[i, ab, pl.ds(aligned((1 - pc.c) * n, 8), n), :],
                    lambda k: out.at[:, cols(pc.c)], lambda k: out.at[:, cols(1 - pc.c)])

    def advance(self, kind, g, out, i, s):
        pc = self.place
        r0, r1, r2, r3, fin = self.bufs[kind]
        if s == 5:
            for ab in range(1 if kind == "r" else 2):
                self.swap(kind, g, out, i, ab, 4).arrive()
            return
        for ab in range(2):
            first, second = ("y", "x") if ab == 0 else ("x", "y")
            if s:
                self.swap(kind, g, out, i, ab, s - 1).arrive()
            if s == 1:
                n = r0.shape[-2]

                def add(z, _):
                    if kind == "r":
                        own = g[z, :, :, ab * n:(ab + 1) * n, lanes(pc.c * (D // 2) + i * 128, 128)]
                    else:
                        own = g[z, :, :, :, lanes(pc.c * FF_HALF + i * 256 + ab * 128, 128)]
                    r0[i, ab, z] = (r0[i, ab, z].astype(F32) + own.astype(F32)).astype(BF16)
                    return 0

                lax.fori_loop(0, pc.nz, add, 0)
            if s == 2:
                at = (every, pc.y, every) if first == "y" else (every, every, pc.x)
                v = r0[(i, ab) + at].astype(F32)
                for k in range(pc.size(first) - 1):
                    v = v + r1[i, ab, k].astype(F32)
                r1[i, ab, 0] = v.astype(BF16)
            if s == 3:
                v = r1[i, ab, 0, :, pc.at(second)].astype(F32)
                for k in range(pc.size(second) - 1):
                    v = v + r2[i, ab, k].astype(F32)
                r2[i, ab, 0] = v.astype(BF16)
            if s == 4:
                v = r2[i, ab, 0, pc.z].astype(F32)
                for k in range(pc.nz - 1):
                    v = v + r3[i, ab, k].astype(F32)
                fin[i, ab] = v
                if kind != "r":
                    n = out.shape[0]
                    out[:, lanes(pc.c * FF_HALF + i * 256 + ab * 128, 128)] = fin[i, ab, pl.ds(aligned(pc.c * n, 8), n), :]
            if s < 4 or kind != "r":
                self.swap(kind, g, out, i, ab, s).start()
        if s == 4 and kind == "r":
            out[:, lanes(pc.c * (D // 2) + i * 128, 128)] = fin[i, pc.c]
            self.swap(kind, g, out, i, 0, 4).start()

    def done(self, kind, g, out, pieces, steps):
        for i in range(pieces):
            for s in steps:
                for ab in range(1 if (kind == "r" and s == 4) else 2):
                    self.swap(kind, g, out, i, ab, s).done()


class SmallSum:
    def __init__(self, place, slots, send, recv):
        self.place, self.slots, self.send, self.recv = place, slots, send, recv

    def base(self, i):
        return sum(self.place.size(a) for a in "cyxz"[:i])

    def swap(self, i):
        pc, a = self.place, "cyxz"[i]
        sems = (lambda k: self.send.at[i, k - 1], lambda k: self.recv.at[i, k - 1])
        me = lambda k: self.slots.at[self.base(i) + pc.at(a)]
        return Swap(pc, a, sems, me, me, lambda k: self.slots.at[self.base(i) + pc.back(a, k)])

    def start(self):
        self.swap(0).start()

    def advance(self, i):
        self.swap(i).arrive()
        s = self.slots[self.base(i)]
        for k in range(1, self.place.size("cyxz"[i])):
            s = s + self.slots[self.base(i) + k]
        if i == 3:
            return s
        self.slots[self.base(i + 1) + self.place.at("cyxz"[i + 1])] = s
        self.swap(i + 1).start()

    def done(self):
        for i in range(4):
            self.swap(i).done()


def events(t):
    out = [("e", i, s) for i in range(6) for s in range(6) if 2 * i + 1 + 2 * s == t and t >= 12]
    for i, at in enumerate(((12, 14, 16, 18, 20, 22), (13, 15, 17, 19, 21, 23), (14, 15, 18, 20, 22, 24))):
        out += [("r", i, s) for s in range(6) if at[s] == t]
    return out + [("t", 5, s) for s in range(6) if 16 + 2 * s == t]


def backward_kernel(near, dims, counts, rasq, do, w, r, own_ew, own_er, triple_h, pt_h, att_h, mixed_h, n2_h, normed_h,
                    xp_h, sv, eb, o_out, o_dx, o_act, o_t, o_e, o_r, o_small, o_deb, o_t4,
                    raster, ew, rw, dop, dn2, mixed, part, e0, e1, e2, e3, ef, t0, t1, t2, t3, tf, b0, b1, b2, b3, bf, slots_a, slots_g, late, slots_l, sums_g, smalls,
                    gsend, grecv, send, recv, ssend, srecv, lsem):
    def load(n, src, dst):
        return pltpu.make_async_copy(src, dst, lsem.at[n])

    if near:
        pc = Place(dims)
        rs = Scatter(pc, {"e": (e0, e1, e2, e3, ef), "t": (t0, t1, t2, t3, tf), "r": (b0, b1, b2, b3, bf)}, send, recv)
        sum_a = SmallSum(pc, slots_a, ssend.at[0], srecv.at[0])
        sum_l = SmallSum(pc, slots_l, ssend.at[1], srecv.at[1])
        sum_g = lambda g: SmallSum(pc, slots_g.at[g], ssend.at[2 + g], srecv.at[2 + g])
        pc.greet()
    else:
        pc = None
    small = smalls
    fill_places(raster)
    small[...] = jnp.zeros(small.shape, F32)

    def feed_forward(n2, n2t, act, hs, ds, hl, de, dr):
        half_z = dims[0] // 2
        loads = [load(0, n2_h, n2), load(3, mixed_h, mixed)]
        if near:
            for c in range(2):
                a, b = lanes(c * HALF + TM_HALF, FF_PART), lanes(c * FF_HALF, FF_PART)
                loads.append(load(4 + c, w.at[:, :, :, :, a], ew.at[:, :, :, :, b]))
            loads.append(load(2, r.at[0:half_z], rw.at[0:half_z]))
        else:
            for c in range(2):
                a, b = lanes(c * HALF + TM_HALF, FF_HALF), lanes(c * FF_HALF, FF_HALF)
                loads.append(load(4 + c, w.at[:, :, :, :, a], ew.at[:, :, :, :, b]))
            loads.append(load(2, r, rw))
        for c in loads:
            c.start()
        if near:
            gather = Gather(pc, ew, FF_HALF, FF_PART, 3, rw, 1, gsend, grecv)
            ew[pc.z, pc.y, pc.x, :, lanes(pc.c * FF_HALF + FF_PART, FF_PART)] = own_ew[...]

            @pl.when(pc.z >= half_z)
            def _():
                rw[pc.z, pc.y, pc.x, :, lanes(pc.c * (D // 2), D // 2)] = own_er[...]

            gather.tick(0, False)
            gather.tick(1, True)

        def permute(i, _):
            dop[window(i), :] = dot(to_window(raster, i % 4), do[i // 4]).astype(BF16)
            return 0

        lax.fori_loop(0, 8, permute, 0)
        for c in loads:
            c.wait()
        n2t[...] = n2[...].T
        dn2[...] = jnp.zeros(dn2.shape, F32)
        small[7:8, :] = jnp.sum(dop[...].astype(F32), axis=0, keepdims=True)
        nz, ny, nx, rr = rw.shape[:4]
        per = FF // 256

        def rows_of(n0):
            return flat_r[pl.ds(aligned(n0, 256), 256), :]

        flat_r = rw.reshape(FF, D)
        fe, fde = Flat(ew), de

        def chunk(j, _):
            s, k = j // 6, j % 6
            c, off = k % 2, k // 2
            col = lanes(c * FF_HALF + s * FF_PART + off * 256, 256)
            n0 = s * FF_HALF + c * FF_PART + off * 256
            nat = lanes(n0, 256)
            weights = fe[:, col]
            rows = rows_of(n0)
            hs[...] = dot(n2[...], weights)
            ds[...] = dot(dop[...], rows, NT)
            bias = eb[0:1, nat]
            total = jnp.zeros((8, 256), F32)
            for m in range(18):
                rr_ = pl.ds(m * 64, 64)
                a, slope = gelu_pair(hs[rr_, :] + bias)
                act[rr_, nat] = a.astype(BF16)
                hg = ds[rr_, :] * slope
                for q in range(8):
                    total = total + hg[q * 8:(q + 1) * 8]
                hl[rr_, :] = hg.astype(BF16)
            small[pl.ds(8 + s * 2 + c, 1), lanes(off * 256, 256)] = jnp.sum(total, axis=0, keepdims=True)
            de[:, :, :, :, col] = dot(n2t[...], hl[...]).astype(BF16).reshape(de.shape[:4] + (256,))
            for n in range(3):
                cc = lanes(n * 256, 256)
                dn2[:, cc] += dot(hl[...], weights[n * 256:(n + 1) * 256], NT)
            if near:
                gather.tick(2 + 2 * j, False)
                gather.tick(3 + 2 * j, True)
                for step in range(5, -1, -1):
                    i = j // 2 - step
                    pl.when(jnp.logical_and(lax.rem(j, 2) == 1, i >= 0))(
                        lambda i=i, step=step: rs.advance("e", de, o_e, i, step))
            return 0

        lax.fori_loop(0, per, chunk, 0)

        def er_tick(t):
            for kind, i, s in events(t):
                rs.advance(kind, de if kind == "e" else dr, o_e if kind == "e" else o_r, i, s)

        spill = load(6, act, o_act)
        spill.start()
        flat_dr = dr.reshape(FF, D)

        def reduce_part(n, _):
            def quarter(m, _):
                two = jnp.concatenate([dop[:, lanes(n * 128, 128)], dop[:, lanes(D // 2 + n * 128, 128)]], axis=1)
                v = dot(act[:, lanes(m * D, D)], two, TN).astype(BF16)
                rows = pl.ds(aligned(m * D, D), D)
                flat_dr[rows, lanes(n * 128, 128)] = v[:, :128]
                flat_dr[rows, lanes(D // 2 + n * 128, 128)] = v[:, 128:]
                return 0

            lax.fori_loop(0, 4, quarter, 0)
            if near:
                for t in range(3):
                    pl.when(n == t)(lambda t=t: er_tick(12 + t))
            return 0

        lax.fori_loop(0, 3, reduce_part, 0)

        def ln2b(i, _):
            rows = window(i)
            hat, inv = stats(mixed[rows, :])
            g = dn2[rows, :]
            small[5:6, :] += jnp.sum(g * hat, axis=0, keepdims=True)
            small[6:7, :] += jnp.sum(g, axis=0, keepdims=True)
            m = dop[rows, :].astype(F32) + norm_back(hat, inv, sv[5:6, :], g)
            small[4:5, :] += jnp.sum(m, axis=0, keepdims=True)
            mixed[rows, :] = m
            part[rows, :] = m.astype(BF16)
            return 0

        lax.fori_loop(0, 8, ln2b, 0)
        if near:
            er_tick(15)
            gather.finish()
            rs.done("e", de, o_e, 6, range(1))
            rs.done("r", dr, o_r, 3, range(1))
        else:
            for c in (load(4, de, o_e), load(5, dr, o_r)):
                c.start()
                c.wait()
        spill.wait()

    nz, ny, nx, rw_rows = w.shape[:4]
    rr_rows = r.shape[3]
    vm = pltpu.VMEM
    pl.run_scoped(feed_forward, vm((ROWS, D), BF16),
                  vm((D, ROWS), BF16), vm((ROWS, FF), BF16), vm((ROWS, 256), F32), vm((ROWS, 256), F32), vm((ROWS, 256), BF16),
                  vm((nz, ny, nx, rw_rows, FF), BF16), vm((nz, ny, nx, rr_rows, D), BF16))
    tw = ew
    flat_tw = tw.reshape(D, FF)
    flat_r = rw.reshape(FF, D)

    def after_feed_forward(dt, triple, ml, xp, t4g, sum_keep):
        def ert_tick(t):
            if near:
                for kind, i, s in events(t):
                    rs.advance(kind, {"e": None, "r": None, "t": dt}[kind], {"e": o_e, "r": o_r, "t": o_t}[kind], i, s)

        def put(parts, v):
            at = 0
            for h, lo, n in parts:
                dt[:, :, :, :, lanes(h * TM_HALF + lo, n)] = v[:, at:at + n].reshape(dt.shape[:4] + (n,))
                at += n

        def group_sum(g, m):
            total = sum_g(g).advance(m)
            if total is not None:
                sums_g[g] = total

        def t_tick(t):
            for s in range(5, -1, -1):
                q = t - 19 - s
                if isinstance(t, int):
                    if q % 2 == 0 and 0 <= q // 2 <= 2:
                        k = q // 2
                        for i in range(3 - k - k // 2, 5 - 2 * k + k // 2):
                            rs.advance("t", dt, o_t, i, s)
                else:
                    k = q // 2

                    def run(k=k, s=s):
                        lax.fori_loop(3 - k - k // 2, 5 - 2 * k + k // 2,
                                      lambda i, _: (rs.advance("t", dt, o_t, i, s), 0)[1], 0)

                    pl.when(jnp.logical_and(q >= 0, lax.rem(q + 20, 2) == 0))(run)

        def attention(datt, xt, xn, qs, dos, st, raw, pt, bgrad, accbuf, psem):
            loads = [load(0, att_h, xn), load(1, triple_h, triple), load(2, xp_h, xp)]
            loads += [load(4 + c, w.at[:, :, :, :, lanes(c * HALF, TM_HALF)], tw.at[:, :, :, :, lanes(c * TM_HALF, TM_HALF)])
                      for c in range(2)]
            for c in loads:
                c.start()

            def fetch(step):
                return pltpu.make_async_copy(pt_h.at[(2 - step // 8) * 8 + step % 8], pt.at[step % 2], psem.at[step % 2])

            fetch(0).start()
            for c in loads:
                c.wait()
            xt[...] = xn[...].T
            again = load(0, normed_h, xn)
            again.start()

            def merge_grad(n, _):
                put(merge_cols(n), dot(xt[...], part[:, lanes(n * 256, 256)]).astype(BF16))
                return 0

            lax.fori_loop(0, 3, merge_grad, 0)
            ert_tick(16)

            def merge_back(n, _):
                rows = pl.ds(aligned(n * 256, 256), 256)
                m = jnp.concatenate([flat_tw[rows, 1152:TM_HALF], flat_tw[rows, TM_HALF + 1152:]], axis=1)
                datt[:, lanes(n * 256, 256)] = dot(part[...], m, NT).astype(BF16)
                return 0

            lax.fori_loop(0, 3, merge_back, 0)
            again.wait()
            xt[...] = xn[...].T
            ert_tick(17)
            if near:
                slots_a[pc.c, 0:4, :] = small[4:8, :]
                slots_a[pc.c, 4:8, :] = small[8:12, :]
                sum_a.start()

            def one(step, g):
                i = step % 8
                b, v = i // 4, i % 4
                rows = window(i)
                col = lambda k: lanes(g * D + k * GW, GW)
                slot = step % 2

                @pl.when(step < 23)
                def _():
                    fetch(step + 1).start()

                valid = raster[v] < counts[b]
                vq = jnp.concatenate([valid, valid], axis=1)
                da = datt[rows, lanes(g * GW, GW)]
                da = jnp.where(vq, da.astype(F32), 0.0).astype(BF16)
                head_stack(qs, triple[rows, col(0)])
                head_stack(dos, da)
                st[...] = dot(triple[rows, col(2)], dos[...], NT)
                fetch(step).wait()
                for n in range(9):
                    c = lanes(n * 128, 128)
                    p = pt[slot, :, c].astype(F32)
                    d = st[:, c]
                    inner = jnp.sum(p * d, axis=0, keepdims=True)
                    s = p * (d - inner)
                    bgrad[n] += s
                    raw[:, c] = (s * SCALE).astype(BF16)
                key = triple[rows, col(1)]
                triple[rows, col(2)] = dot(pt[slot], dos[...]).astype(BF16)
                triple[rows, col(1)] = dot(raw[...], qs[...]).astype(BF16)
                triple[rows, col(0)] = head_pick(dot(raw[...], key, TN)).astype(BF16)

            def half_group(q, _):
                g = 2 - q // 2

                @pl.when(q % 2 == 0)
                def _():
                    bgrad[...] = jnp.zeros(bgrad.shape, F32)

                lax.fori_loop(0, 4, lambda j, _: (one(q * 4 + j, g), 0)[1], 0)

                @pl.when(q % 2 == 1)
                def _():
                    gather_bias(g, bgrad, accbuf, t4g)
                    for k, parts in enumerate(group_cols(g)):
                        v = triple[:, lanes(g * D + k * GW, GW)]
                        if k != 1:
                            small[2 + k // 2:3 + k // 2, lanes(g * GW, GW)] = jnp.sum(v.astype(F32), axis=0, keepdims=True)
                        put(parts, dot(xt[...], v).astype(BF16))

                if near:
                    for t in range(18, 24):
                        if events(t):
                            pl.when(q == t - 18)(lambda t=t: ert_tick(t))
                    t_tick(18 + q)
                    for m in range(4):
                        k = (q - 2 - m) // 2

                        def more(k=k, m=m):
                            total = sum_g(2 - k).advance(m)
                            if total is not None:
                                sums_g[2 - k] = total

                        pl.when(jnp.logical_and(q - 2 - m >= 0, lax.rem(q + 10 - m, 2) == 0))(more)
                    for m, at in enumerate((0, 2, 4)):
                        pl.when(q == at)(lambda m=m: sum_a.advance(m) and None)

                    @pl.when(q % 2 == 1)
                    def _():
                        own = slots_g.at[g, pc.c]
                        own[...] = jnp.zeros(own.shape, F32)
                        own[0:8, 0:4 * WT] = t4g[pl.ds(aligned(g * GH, GH), GH), :]
                        for k in range(2):
                            own[8 + k:9 + k, 0:GW] = small[2 + k:3 + k, lanes(g * GW, GW)]
                        sum_g(g).start()
                return 0

            lax.fori_loop(0, 2 * GROUPS, half_group, 0)
        def rest(act):
            again = load(0, o_act, act)
            again.start()

            def normed_grad(n, _):
                rows = pl.ds(aligned(n * 256, 256), 256)
                weights = jnp.concatenate([flat_tw[rows, h * TM_HALF + lo:h * TM_HALF + lo + m]
                                           for g in range(GROUPS) for p in group_cols(g) for h, lo, m in p], axis=1)
                dn2[:, lanes(n * 256, 256)] = dot(triple[...], weights, NT)
                if near:
                    for t in range(2):
                        @pl.when(n == t)
                        def _(t=t):
                            ert_tick(24 + t)
                            t_tick(24 + t)
                            group_sum(0, t)
                            group_sum(1, t + 2)
                return 0

            lax.fori_loop(0, 3, normed_grad, 0)

            def ln1b(i, _):
                rows = window(i)
                hat, inv = stats(xp[rows, :].astype(F32))
                g = dn2[rows, :]
                late[0:1, :] += jnp.sum(g * hat, axis=0, keepdims=True)
                late[1:2, :] += jnp.sum(g, axis=0, keepdims=True)
                ml[rows, :] = (mixed[rows, :] + norm_back(hat, inv, sv[0:1, :], g)).astype(BF16)
                return 0

            late[...] = jnp.zeros(late.shape, F32)
            lax.fori_loop(0, 8, ln1b, 0)
            if near:
                slots_l[pc.c] = late[0:2, :]
                sum_l.start()
                ert_tick(26)
                t_tick(26)
                group_sum(0, 2)
                sum_keep[...] = sum_a.advance(3)
            mixed_again = load(3, mixed_h, mixed)
            mixed_again.start()

            def back_to_raster(src, dst):
                def block(k, _):
                    b, m = k // 4, k % 4
                    dst[window(k), :] = dot(to_raster(rasq, m), src[pl.ds(aligned(b * TOK, TOK), TOK), :]).astype(BF16)
                    return 0

                lax.fori_loop(0, 8, block, 0)

            back_to_raster(ml, part)
            saves = [load(4 + b, part.at[b * TOK:(b + 1) * TOK, :], o_dx.at[b]) for b in range(2)]
            for c in saves:
                c.start()
            if near:
                t_tick(27)
                group_sum(0, 3)
                sum_l.advance(0)
            again.wait()
            mixed_again.wait()

            def output(n, _):
                c = lanes(n * 256, 256)
                ml[:, c] = (mixed[:, c] + dot(act[...], flat_r[:, c]) + sv[7:8, c]).astype(BF16)
                if near:
                    for t in range(2):
                        @pl.when(n == t)
                        def _(t=t):
                            t_tick(28 + t)
                            sum_l.advance(1 + t)
                return 0

            lax.fori_loop(0, 3, output, 0)
            back_to_raster(ml, dop)
            more = [load(b, dop.at[b * TOK:(b + 1) * TOK, :], o_out.at[b]) for b in range(2)]
            for c in more:
                c.start()
            if near:
                total_l = sum_l.advance(3)
                dev = pc.z * (2 * pc.ny * pc.nx) + (pc.y * pc.nx + pc.x) * 2 + pc.c
                n = o_small.shape[1]
                shift = lax.rem(D - dev * n, D)
                biases = [jnp.concatenate([sums_g[g, 8 + k:9 + k, 0:GW] for g in range(GROUPS)], axis=1) for k in range(2)]
                rows = jnp.concatenate([total_l] + biases + [sum_keep[0:4, :]], axis=0)
                o_small[...] = pltpu.roll(rows, shift, axis=1)[:, 0:n]
                wide_n = o_deb.shape[1]
                per = D // wide_n
                row = sum_keep[pl.ds(4 + dev // per, 1), :]
                o_deb[...] = pltpu.roll(row, lax.rem(D - lax.rem(dev, per) * wide_n, D), axis=1)[:, 0:wide_n]
                for g in range(GROUPS):
                    o_t4[g * GH:(g + 1) * GH, :] = sums_g[g, 0:8, 0:4 * WT]
                rs.done("e", None, o_e, 6, range(1, 5))
                rs.done("r", None, o_r, 3, range(1, 5))
                rs.done("t", dt, o_t, 6, range(5))
                sum_a.done()
                sum_l.done()
                for g in range(GROUPS):
                    sum_g(g).done()
            else:
                o_small[0:2, :] = late[0:2]
                o_small[2:8, :] = small[2:8, :]
                for k in range(4):
                    o_deb[0:1, k * D:(k + 1) * D] = small[8 + k:9 + k, :]
                o_t4[...] = t4g[...]
                save = load(3, dt, o_t)
                save.start()
                save.wait()
            for c in saves + more:
                c.wait()

        pl.run_scoped(attention, vm((ROWS, D), BF16), vm((D, ROWS), BF16), vm((ROWS, D), BF16), vm((QL, GW), BF16),
                      vm((QL, GW), BF16), vm((WT, QL), F32), vm((WT, QL), BF16), vm((2, WT, QL), BF16), vm((9, WT, 128), F32),
                      vm((2, 16, QL), F32), pltpu.SemaphoreType.DMA((2,)))
        pl.run_scoped(rest, vm((ROWS, FF), BF16))

    pl.run_scoped(after_feed_forward, vm((nz, ny, nx, rw_rows, 2 * TM_HALF), BF16), vm((ROWS, 3 * D), BF16),
                  vm((ROWS, D), BF16), vm((ROWS, D), BF16), vm((HEADS, 4 * WT), F32), vm((8, D), F32))


def backward(near, dims, counts, do, w, r, own_ew, own_er, triple, pt, att, mixed, n2, normed, xp, sv, eb):
    nz, ny, nx = dims if near else (1, 1, 1)
    if not near:
        w, r = w.reshape(1, 1, 1, D, -1), r.reshape(1, 1, 1, FF, D)
    rw, rr = w.shape[3], r.shape[3]
    peers = max(nz, ny, nx, 2) - 1
    vm = pltpu.VMEM
    dma = pltpu.SemaphoreType.DMA
    bufs = []
    for count, n in ((6, rw), (6, rw), (3, rr // 2)) if near else ((1, 16),) * 3:
        bufs += [vm((count, 2, nz, ny, nx, n, 128), BF16), vm((count, 2, max(ny - 1, 1), nz, nx, n, 128), BF16),
                 vm((count, 2, max(nx - 1, 1), nz, n, 128), BF16), vm((count, 2, max(nz - 1, 1), n, 128), BF16),
                 vm((count, 2, n, 128), F32)]
    n_slots = 2 + nz + ny + nx
    if near:
        outs = [((rw // 2, 2 * TM_HALF), F32), ((rw // 2, FF), F32), ((rr // 2, D), F32), ((8, rw // 2), F32), ((1, rr // 2), F32)]
    else:
        outs = [((1, 1, 1, D, 2 * TM_HALF), BF16), ((1, 1, 1, D, FF), BF16), ((1, 1, 1, FF, D), BF16), ((8, D), F32), ((1, FF), F32)]
    outs = [((2, TOK, D), BF16), ((2, TOK, D), BF16), ((ROWS, FF), BF16)] + outs + [((HEADS, 4 * WT), F32)]
    params = dict(collective_id=1, has_side_effects=True) if near else {}
    return pl.pallas_call(
        functools.partial(backward_kernel, near, dims),
        out_shape=[jax.ShapeDtypeStruct(s, d) for s, d in outs],
        in_specs=[SM, VM, VM, ANY, ANY, VM, VM] + [ANY] * 7 + [VM] * 2,
        out_specs=[ANY] * 3 + ([VM] * 3 if near else [ANY] * 3) + [VM] * 3,
        scratch_shapes=[vm((4, WT, 128), jnp.int32), vm((nz, ny, nx, rw, FF), BF16), vm((nz, ny, nx, rr, D), BF16), vm((ROWS, D), BF16), vm((ROWS, D), F32),
                        vm((ROWS, D), F32), vm((ROWS, D), BF16)] + bufs
        + [vm((n_slots, 8, D), F32), vm((GROUPS, n_slots, 16, 640), F32), vm((8, D), F32), vm((n_slots, 2, D), F32),
           vm((GROUPS, 16, 640), F32), vm((16, D), F32),
           dma((6, 4, peers)), dma((6, 4, peers)), dma((15, 2, 5, peers)), dma((15, 2, 5, peers)), dma((5, 4, peers)),
           dma((5, 4, peers)), dma((7,))],
        name="backward",
        compiler_params=pltpu.CompilerParams(vmem_limit_bytes=VMEM_LIMIT, **params),
    )(counts, jnp.asarray(RASTER_Q), do, w, r, own_ew, own_er, triple, pt, att, mixed, n2, normed, xp, sv,
      eb)


def finish_kernel(target, out_h, dx_h, t, e, r, small, deb, t4, out, dx, triple, merge, expand, reduce, table, *rest):
    vectors = rest
    out[...] = out_h[...]
    dx[...] = dx_h[...]
    for g in range(GROUPS):
        for k, parts in enumerate(group_cols(g)):
            at = k * D + g * GW
            for h, lo, n in parts:
                triple[:, at:at + n] = t[:, h * TM_HALF + lo:h * TM_HALF + lo + n]
                at += n
    for c in range(2):
        merge[:, c * D // 2:(c + 1) * D // 2] = t[:, c * TM_HALF + 1152:(c + 1) * TM_HALF]
        for s in range(2):
            expand[:, s * FF_HALF + c * FF_PART:s * FF_HALF + (c + 1) * FF_PART] = (
                e[:, c * FF_HALF + s * FF_PART:c * FF_HALF + (s + 1) * FF_PART])
    reduce[...] = r[...]
    for k, v in enumerate(vectors[:8]):
        v[...] = small[k, :]
    vectors[8][...] = deb[0, :]
    table[...] = lax.dot_general(t4[...], onehot(target), NT, precision=lax.Precision.HIGHEST,
                                 preferred_element_type=F32)


def weights_in_pieces(triple_weight, merge_weight, expand_weight):
    halves = []
    for c in range(2):
        for g in range(GROUPS):
            q, k, v = (triple_weight[:, i * D + g * GW:i * D + (g + 1) * GW] for i in range(3))
            halves += [q, k[:, :128]] if c == 0 else [k[:, 128:], v]
        halves.append(merge_weight[:, c * D // 2:(c + 1) * D // 2])
        halves += [expand_weight[:, s * FF_HALF + c * FF_PART:s * FF_HALF + (c + 1) * FF_PART] for s in range(2)]
    return jnp.concatenate(halves, axis=1)


def shards(dims, block_input, valid_counts, output_cotangent, triple_weight, merge_weight, expand_weight, reduce_weight,
           first_gain, first_shift, query_bias, value_bias, merge_bias, second_gain, second_shift, expand_bias,
           reduce_bias, position_table):
    counts = valid_counts[:, 0]
    rows = triple_weight.shape[0]
    near = rows % 8 == 0 and dims[0] % 4 == 0 and dims[1] == dims[2]
    if near:
        given = (triple_weight, merge_weight, expand_weight, reduce_weight, first_gain, first_shift, query_bias, value_bias,
                 merge_bias, second_gain, second_shift, reduce_bias, expand_bias)
    else:
        small = jnp.stack([first_gain, first_shift, query_bias, value_bias, merge_bias, second_gain, second_shift,
                           reduce_bias])
        gather = lambda v, axis: lax.all_gather(v.astype(BF16), AXES, axis=axis, tiled=True)
        given = (gather(weights_in_pieces(triple_weight, merge_weight, expand_weight), 0), gather(reduce_weight, 0),
                 gather(small, 1).astype(F32), jnp.broadcast_to(gather(expand_bias, 0).astype(F32)[None], (8, FF)))
    o_w, o_r, triple, pt, att, mixed, n2, normed, xp, sv, eb, own_ew, own_er = forward(
        near, dims, counts, block_input[:, 0], position_table, *given)
    if not near:
        o_w, o_r = given[:2]
    out, dx, _, gt, ge, gr, gs, gb, t4 = backward(near, dims, counts, output_cotangent[:, 0], o_w, o_r, own_ew, own_er, triple, pt,
                                               att, mixed, n2, normed, xp, sv, eb)
    if not near:
        scatter = lambda v, axis: lax.psum_scatter(v.astype(F32), AXES, scatter_dimension=axis, tiled=True)
        gt, ge, gr = scatter(gt.reshape(D, -1), 0), scatter(ge.reshape(D, -1), 0), scatter(gr.reshape(FF, D), 0)
        gs, gb, t4 = scatter(gs, 1), scatter(gb, 1), lax.psum(t4, AXES)
    n, rr = expand_bias.shape[0], reduce_weight.shape[0]
    image = jax.ShapeDtypeStruct((2, TOK, D), BF16)
    shapes = [(rows, 3 * D), (rows, D), (rows, FF), (rr, D), (HEADS, EXT * EXT)] + [(rows,)] * 8 + [(n,)]
    out, dx, tr, mg, ex, re, table, *vec = pl.pallas_call(
        finish_kernel, out_shape=[image, image] + [jax.ShapeDtypeStruct(s, F32) for s in shapes],
        in_specs=[VM] * 9, out_specs=[VM] * (2 + len(shapes)), name="finish",
        compiler_params=pltpu.CompilerParams(vmem_limit_bytes=VMEM_LIMIT),
    )(jnp.asarray(TARGET), out, dx, gt, ge, gr, gs, gb, t4)
    return (out[:, None], dx[:, None], tr, mg, ex, re, *vec[:7], vec[8], vec[7], table.T)


def solution(mesh):
    image = P(None, AXES, None, None)
    rows = P(AXES, None)
    vec = P(AXES)
    return jax.shard_map(
        functools.partial(shards, mesh_dims(mesh)), mesh=mesh,
        in_specs=(image, P(None, AXES), image) + (rows,) * 4 + (vec,) * 9 + (P(),),
        out_specs=(image, image) + (rows,) * 4 + (vec,) * 9 + (P(),),
        check_vma=False)
```

profile of v0, /device:TPU:0, one launch (start us, length us, event | category | flops | bytes accessed | tf_op | source)
XLA Modules:
  0.0 250.5 jit_solution(9365633864328148517)
XLA Ops:
  0.7 77.9 %forward.1 = (bf16[4,2,2,48,6144]{4,3,2,1,0:T(8,128)(2,1)}, bf16[4,2,2,192,768]{4,3,2,1,0:T(8,128)(2,1)}, bf16[1152,2304]{1,0:T(8,128)(2,1)}, bf16[24,144,1152]{...) custom-call(s32[2]{0:T(128)} %bitcast.14, ...), custom_call_target="tpu_custom_call" | custom-call | tf_op jit(solution)/shard_map/forward/pallas_call | solution.py:660
  78.6 166.2 %backward.1 = (bf16[2,576,768]{2,1,0:T(8,128)(2,1)}, bf16[2,576,768]{2,1,0:T(8,128)(2,1)}, bf16[1152,3072]{1,0:T(8,128)(2,1)}, f32[24,3072]{1,0:T(8,128)}, f32[2...) custom-call(s32[2]{0:T(128)} %bitcast.15, ...), custom_call_target="tpu_custom_call" | custom-call | tf_op jit(solution)/shard_map/backward/pallas_call | solution.py:1253
  244.8 5.6 %finish.1 = (bf16[2,576,768]{2,1,0:T(8,128)(2,1)}, bf16[2,576,768]{2,1,0:T(8,128)(2,1)}, f32[24,2304]{1,0:T(8,128)}, f32[24,768]{1,0:T(8,128)}, f32[24,3072]{1,0...) custom-call(s32[8,576]{1,0:T(8,128)} %constant.7.clone.target, ...), custom_call_target="tpu_custom_call" | custom-call | tf_op jit(solution)/shard_map/finish/pallas_call | solution.py:1332
where the time goes:
time: 251 us
  Pallas kernels  250 us (100%)
    pallas_call x1, Pallas kernels, backward(): pl.pallas_call(functools.partial(backward_kernel, near, dims), out_shape=...  166 us
    pallas_call x1, Pallas kernels, forward(): pl.pallas_call(functools.partial(forward_kernel, near, dims), out_shape=[...  77.9 us
    pallas_call x1, Pallas kernels, shards(): pl.pallas_call(finish_kernel, out_shape=[image, image] + [jax.ShapeDtypeS...  5.58 us

commit v1 on v0

--- a/solution.py
+++ b/solution.py
@@ -552,25 +552,27 @@
     keep(25, normed, o_normed).start()
     wf = Flat(w)
 
-    def attn(t, i, g):
-        b, v = i // 4, i % 4
-        rows = window(i)
-        col = lambda k: lanes(g * D + k * GW, GW)
-        valid = raster[v] < counts[b]
-        lk[...] = jnp.where(valid, labk[v], -1)
-        head_stack(qs, triple[rows, col(0)])
-        st[...] = dot(triple[rows, col(1)], qs[...], NT)
-        slot = t % 2
+    def products(i, g, u):
+        rows, v = window(i), i % 4
+        lk[u] = jnp.where(raster[v] < counts[i // 4], labk[v], -1)
+        head_stack(qs.at[u], triple[rows, lanes(g * D, GW)])
+        st[u] = dot(triple[rows, lanes(g * D + GW, GW)], qs[u], NT)
+
+    def softmax(i, g, u):
         for n in range(9):
             c = lanes(n * 128, 128)
-            s = st[:, c] + bias[g * 9 + n]
-            s = jnp.where(lk[...] == labq[v, 0:1, c], s, MASKED)
+            s = st[u, :, c] + bias[g * 9 + n]
+            s = jnp.where(lk[u] == labq[i % 4, 0:1, c], s, MASKED)
             m = jnp.max(s, axis=0, keepdims=True)
             e = jnp.exp((s - m) * SCALE)
             tot = jnp.sum(e, axis=0, keepdims=True)
-            pt[slot, :, c] = (e * (1.0 / tot)).astype(BF16)
-        pltpu.make_async_copy(pt.at[slot], o_pt.at[g * 8 + i], psem.at[slot]).start()
-        out = head_pick(dot(pt[slot], triple[rows, col(2)], TN))
+            pt[u, :, c] = (e * (1.0 / tot)).astype(BF16)
+
+    def attend(i, g, u):
+        rows = window(i)
+        pltpu.make_async_copy(pt.at[u], o_pt.at[g * 8 + i], psem.at[u]).start()
+        out = head_pick(dot(pt[u], triple[rows, lanes(g * D + 2 * GW, GW)], TN))
+        valid = raster[i % 4] < counts[i // 4]
         vq = jnp.concatenate([valid, valid], axis=1)
         attended[rows, lanes(g * GW, GW)] = jnp.where(vq, out, 0.0).astype(BF16)
 
@@ -585,17 +587,18 @@
                     v = v + sv[2 + k // 2:3 + k // 2, lanes(g * GW, GW)]
                 triple[:, lanes(g * D + k * GW, GW)] = v.astype(BF16)
 
-        def one(j, _):
-            step = q * 2 + j
-
-            @pl.when(step >= 2)
-            def _():
-                pltpu.make_async_copy(pt.at[step % 2], o_pt.at[0], psem.at[step % 2]).wait()
-
-            attn(step, step % 8, g)
-            return 0
-
-        lax.fori_loop(0, 2, one, 0)
+        @pl.when(q >= 1)
+        def _():
+            for u in range(2):
+                pltpu.make_async_copy(pt.at[u], o_pt.at[0], psem.at[u]).wait()
+
+        i = 2 * lax.rem(q, 4)
+        products(i, g, 0)
+        products(i + 1, g, 1)
+        softmax(i, g, 0)
+        attend(i, g, 0)
+        softmax(i + 1, g, 1)
+        attend(i + 1, g, 1)
         if near:
             for odd in range(2):
                 pl.when(q % 2 == odd)(lambda odd=odd: gather.tick(10 + q, odd == 1, landed))
@@ -653,8 +656,8 @@
     scratch = [vm(full_w, BF16), vm(full_r, BF16), vm((nz, ny, nx, 2, 16, 128), F32), vm((rw if near else 8, HALF), F32),
                vm((rr if near else 8, D // 2), F32), vm((ROWS, D), BF16), vm((ROWS, D), BF16), vm((ROWS, 3 * D), BF16),
                vm((ROWS, D), BF16), vm((ROWS, D), F32), vm((ROWS, D), BF16), vm((2, WT, QL), BF16),
-               vm((HEADS, 4 * WT), F32), vm((GROUPS * 9, WT, 128), F32), vm((2, 16, QL), F32), vm((QL, GW), BF16),
-               vm((WT, QL), F32), vm((WT, 128), jnp.int32), vm((4, WT, 128), jnp.int32), vm((4, WT, 128), jnp.int32),
+               vm((HEADS, 4 * WT), F32), vm((GROUPS * 9, WT, 128), F32), vm((2, 16, QL), F32), vm((2, QL, GW), BF16),
+               vm((2, WT, QL), F32), vm((2, WT, 128), jnp.int32), vm((4, WT, 128), jnp.int32), vm((4, WT, 128), jnp.int32),
                dma((12, 4, peers)), dma((12, 4, peers)), dma((14, peers)), dma((14, peers)), dma((30,)), dma((2,))]
     params = dict(collective_id=0, has_side_effects=True) if near else {}
     return pl.pallas_call(
@@ -797,7 +800,10 @@
     out = [("e", i, s) for i in range(6) for s in range(6) if 2 * i + 1 + 2 * s == t and t >= 12]
     for i, at in enumerate(((12, 14, 16, 18, 20, 22), (13, 15, 17, 19, 21, 23), (14, 15, 18, 20, 22, 24))):
         out += [("r", i, s) for s in range(6) if at[s] == t]
-    return out + [("t", 5, s) for s in range(6) if 16 + 2 * s == t]
+    for pieces, at in (((5,), (16, 18, 20, 22, 24, 26)), ((3, 4), (19, 20, 22, 23, 25, 26)), ((2,), (21, 22, 24, 25, 27, 28)),
+                       ((0, 1), (23, 24, 26, 27, 29, 30))):
+        out += [("t", i, s) for i in pieces for s in range(6) if at[s] == t]
+    return sorted(out, key=lambda e: -e[2])
 
 
 def backward_kernel(near, dims, counts, rasq, do, w, r, own_ew, own_er, triple_h, pt_h, att_h, mixed_h, n2_h, normed_h,
@@ -851,6 +857,9 @@
             return 0
 
         lax.fori_loop(0, 8, permute, 0)
+        if near:
+            gather.tick(2, False)
+            gather.tick(3, True)
         for c in loads:
             c.wait()
         n2t[...] = n2[...].T
@@ -873,26 +882,38 @@
             nat = lanes(n0, 256)
             weights = fe[:, col]
             rows = rows_of(n0)
-            hs[...] = dot(n2[...], weights)
-            ds[...] = dot(dop[...], rows, NT)
             bias = eb[0:1, nat]
             total = jnp.zeros((8, 256), F32)
-            for m in range(18):
-                rr_ = pl.ds(m * 64, 64)
-                a, slope = gelu_pair(hs[rr_, :] + bias)
-                act[rr_, nat] = a.astype(BF16)
-                hg = ds[rr_, :] * slope
-                for q in range(8):
-                    total = total + hg[q * 8:(q + 1) * 8]
-                hl[rr_, :] = hg.astype(BF16)
+
+            def products(m):
+                rows_m = pl.ds(m * 288, 288)
+                hs[rows_m, :] = dot(n2[rows_m, :], weights)
+                ds[rows_m, :] = dot(dop[rows_m, :], rows, NT)
+
+            def gate(m, total):
+                for q in range(288 // 32):
+                    rr_ = pl.ds(m * 288 + q * 32, 32)
+                    a, slope = gelu_pair(hs[rr_, :] + bias)
+                    act[rr_, nat] = a.astype(BF16)
+                    hg = ds[rr_, :] * slope
+                    for p in range(4):
+                        total = total + hg[p * 8:(p + 1) * 8]
+                    hl[rr_, :] = hg.astype(BF16)
+                return total
+
+            products(0)
+            for m in range(4):
+                if m + 1 < 4:
+                    products(m + 1)
+                total = gate(m, total)
             small[pl.ds(8 + s * 2 + c, 1), lanes(off * 256, 256)] = jnp.sum(total, axis=0, keepdims=True)
             de[:, :, :, :, col] = dot(n2t[...], hl[...]).astype(BF16).reshape(de.shape[:4] + (256,))
             for n in range(3):
                 cc = lanes(n * 256, 256)
                 dn2[:, cc] += dot(hl[...], weights[n * 256:(n + 1) * 256], NT)
             if near:
-                gather.tick(2 + 2 * j, False)
-                gather.tick(3 + 2 * j, True)
+                gather.tick(4 + 2 * j, False)
+                gather.tick(5 + 2 * j, True)
                 for step in range(5, -1, -1):
                     i = j // 2 - step
                     pl.when(jnp.logical_and(lax.rem(j, 2) == 1, i >= 0))(
@@ -977,23 +998,6 @@
             if total is not None:
                 sums_g[g] = total
 
-        def t_tick(t):
-            for s in range(5, -1, -1):
-                q = t - 19 - s
-                if isinstance(t, int):
-                    if q % 2 == 0 and 0 <= q // 2 <= 2:
-                        k = q // 2
-                        for i in range(3 - k - k // 2, 5 - 2 * k + k // 2):
-                            rs.advance("t", dt, o_t, i, s)
-                else:
-                    k = q // 2
-
-                    def run(k=k, s=s):
-                        lax.fori_loop(3 - k - k // 2, 5 - 2 * k + k // 2,
-                                      lambda i, _: (rs.advance("t", dt, o_t, i, s), 0)[1], 0)
-
-                    pl.when(jnp.logical_and(q >= 0, lax.rem(q + 20, 2) == 0))(run)
-
         def attention(datt, xt, xn, qs, dos, st, raw, pt, bgrad, accbuf, psem):
             loads = [load(0, att_h, xn), load(1, triple_h, triple), load(2, xp_h, xp)]
             loads += [load(4 + c, w.at[:, :, :, :, lanes(c * HALF, TM_HALF)], tw.at[:, :, :, :, lanes(c * TM_HALF, TM_HALF)])
@@ -1002,9 +1006,10 @@
                 c.start()
 
             def fetch(step):
-                return pltpu.make_async_copy(pt_h.at[(2 - step // 8) * 8 + step % 8], pt.at[step % 2], psem.at[step % 2])
+                return pltpu.make_async_copy(pt_h.at[(2 - step // 8) * 8 + step % 8], pt.at[step % 4], psem.at[step % 4])
 
             fetch(0).start()
+            fetch(1).start()
             for c in loads:
                 c.wait()
             xt[...] = xn[...].T
@@ -1033,37 +1038,53 @@
                 slots_a[pc.c, 4:8, :] = small[8:12, :]
                 sum_a.start()
 
-            def one(step, g):
+            def place_of(step):
                 i = step % 8
-                b, v = i // 4, i % 4
-                rows = window(i)
-                col = lambda k: lanes(g * D + k * GW, GW)
-                slot = step % 2
-
-                @pl.when(step < 23)
-                def _():
-                    fetch(step + 1).start()
-
-                valid = raster[v] < counts[b]
+                return window(i), raster[i % 4] < counts[i // 4]
+
+            def products(step, g, u):
+                rows, valid = place_of(step)
                 vq = jnp.concatenate([valid, valid], axis=1)
                 da = datt[rows, lanes(g * GW, GW)]
                 da = jnp.where(vq, da.astype(F32), 0.0).astype(BF16)
-                head_stack(qs, triple[rows, col(0)])
-                head_stack(dos, da)
-                st[...] = dot(triple[rows, col(2)], dos[...], NT)
-                fetch(step).wait()
+                head_stack(qs.at[u], triple[rows, lanes(g * D, GW)])
+                head_stack(dos.at[u], da)
+                st[u] = dot(triple[rows, lanes(g * D + 2 * GW, GW)], dos[u], NT)
+
+            def softmax_back(slot, u):
                 for n in range(9):
                     c = lanes(n * 128, 128)
                     p = pt[slot, :, c].astype(F32)
-                    d = st[:, c]
+                    d = st[u, :, c]
                     inner = jnp.sum(p * d, axis=0, keepdims=True)
                     s = p * (d - inner)
                     bgrad[n] += s
-                    raw[:, c] = (s * SCALE).astype(BF16)
+                    raw[u, :, c] = (s * SCALE).astype(BF16)
+
+            def grads(step, g, slot, u):
+                rows, _ = place_of(step)
+                col = lambda k: lanes(g * D + k * GW, GW)
                 key = triple[rows, col(1)]
-                triple[rows, col(2)] = dot(pt[slot], dos[...]).astype(BF16)
-                triple[rows, col(1)] = dot(raw[...], qs[...]).astype(BF16)
-                triple[rows, col(0)] = head_pick(dot(raw[...], key, TN)).astype(BF16)
+                triple[rows, col(2)] = dot(pt[slot], dos[u]).astype(BF16)
+                triple[rows, col(1)] = dot(raw[u], qs[u]).astype(BF16)
+                triple[rows, col(0)] = head_pick(dot(raw[u], key, TN)).astype(BF16)
+
+            def pair(p, g):
+                step, slot = 2 * p, 2 * lax.rem(p, 2)
+
+                @pl.when(p < 11)
+                def _():
+                    fetch(step + 2).start()
+                    fetch(step + 3).start()
+
+                products(step, g, 0)
+                products(step + 1, g, 1)
+                fetch(step).wait()
+                fetch(step + 1).wait()
+                softmax_back(slot, 0)
+                grads(step, g, slot, 0)
+                softmax_back(slot + 1, 1)
+                grads(step + 1, g, slot + 1, 1)
 
             def half_group(q, _):
                 g = 2 - q // 2
@@ -1072,7 +1093,7 @@
                 def _():
                     bgrad[...] = jnp.zeros(bgrad.shape, F32)
 
-                lax.fori_loop(0, 4, lambda j, _: (one(q * 4 + j, g), 0)[1], 0)
+                lax.fori_loop(0, 2, lambda j, _: (pair(q * 2 + j, g), 0)[1], 0)
 
                 @pl.when(q % 2 == 1)
                 def _():
@@ -1087,7 +1108,6 @@
                     for t in range(18, 24):
                         if events(t):
                             pl.when(q == t - 18)(lambda t=t: ert_tick(t))
-                    t_tick(18 + q)
                     for m in range(4):
                         k = (q - 2 - m) // 2
 
@@ -1125,9 +1145,9 @@
                         @pl.when(n == t)
                         def _(t=t):
                             ert_tick(24 + t)
-                            t_tick(24 + t)
-                            group_sum(0, t)
                             group_sum(1, t + 2)
+                            if t == 1:
+                                group_sum(0, 0)
                 return 0
 
             lax.fori_loop(0, 3, normed_grad, 0)
@@ -1147,8 +1167,7 @@
                 slots_l[pc.c] = late[0:2, :]
                 sum_l.start()
                 ert_tick(26)
-                t_tick(26)
-                group_sum(0, 2)
+                group_sum(0, 1)
                 sum_keep[...] = sum_a.advance(3)
             mixed_again = load(3, mixed_h, mixed)
             mixed_again.start()
@@ -1166,8 +1185,8 @@
             for c in saves:
                 c.start()
             if near:
-                t_tick(27)
-                group_sum(0, 3)
+                ert_tick(27)
+                group_sum(0, 2)
                 sum_l.advance(0)
             again.wait()
             mixed_again.wait()
@@ -1179,7 +1198,9 @@
                     for t in range(2):
                         @pl.when(n == t)
                         def _(t=t):
-                            t_tick(28 + t)
+                            ert_tick(28 + t)
+                            if t == 0:
+                                group_sum(0, 3)
                             sum_l.advance(1 + t)
                 return 0
 
@@ -1189,6 +1210,7 @@
             for c in more:
                 c.start()
             if near:
+                ert_tick(30)
                 total_l = sum_l.advance(3)
                 dev = pc.z * (2 * pc.ny * pc.nx) + (pc.y * pc.nx + pc.x) * 2 + pc.c
                 n = o_small.shape[1]
@@ -1221,9 +1243,9 @@
             for c in saves + more:
                 c.wait()
 
-        pl.run_scoped(attention, vm((ROWS, D), BF16), vm((D, ROWS), BF16), vm((ROWS, D), BF16), vm((QL, GW), BF16),
-                      vm((QL, GW), BF16), vm((WT, QL), F32), vm((WT, QL), BF16), vm((2, WT, QL), BF16), vm((9, WT, 128), F32),
-                      vm((2, 16, QL), F32), pltpu.SemaphoreType.DMA((2,)))
+        pl.run_scoped(attention, vm((ROWS, D), BF16), vm((D, ROWS), BF16), vm((ROWS, D), BF16), vm((2, QL, GW), BF16),
+                      vm((2, QL, GW), BF16), vm((2, WT, QL), F32), vm((2, WT, QL), BF16), vm((4, WT, QL), BF16),
+                      vm((9, WT, 128), F32), vm((2, 16, QL), F32), pltpu.SemaphoreType.DMA((4,)))
         pl.run_scoped(rest, vm((ROWS, FF), BF16))
 
     pl.run_scoped(after_feed_forward, vm((nz, ny, nx, rw_rows, 2 * TM_HALF), BF16), vm((ROWS, 3 * D), BF16),

time: 251 us -> 242 us (0.964)
  Pallas kernels: 250 us -> 241 us
    pallas_call x1, Pallas kernels: 166 us -> 159 us  [backward(): pl.pallas_call(functools.partial(backward_kernel, near, dims), out_shape=...]
where the time goes in v1:
time: 242 us
  Pallas kernels  241 us (100%)
    pallas_call x1, Pallas kernels, backward(): pl.pallas_call(functools.partial(backward_kernel, near, dims), out_shape=...  159 us
    pallas_call x1, Pallas kernels, forward(): pl.pallas_call(functools.partial(forward_kernel, near, dims), out_shape=[...  76.8 us
    pallas_call x1, Pallas kernels, shards(): pl.pallas_call(finish_kernel, out_shape=[image, image] + [jax.ShapeDtypeS...  5.58 us

profile of v1, /device:TPU:0, one launch (start us, length us, event | category | flops | bytes accessed | tf_op | source)
XLA Modules:
  0.0 242.1 jit_solution(17810494718709981734)
XLA Ops:
  0.7 76.8 %forward.1 = (bf16[4,2,2,48,6144]{4,3,2,1,0:T(8,128)(2,1)}, bf16[4,2,2,192,768]{4,3,2,1,0:T(8,128)(2,1)}, bf16[1152,2304]{1,0:T(8,128)(2,1)}, bf16[24,144,1152]{...) custom-call(s32[2]{0:T(128)} %bitcast.14, ...), custom_call_target="tpu_custom_call" | custom-call | tf_op jit(solution)/shard_map/forward/pallas_call | solution.py:663
  77.4 158.8 %backward.1 = (bf16[2,576,768]{2,1,0:T(8,128)(2,1)}, bf16[2,576,768]{2,1,0:T(8,128)(2,1)}, bf16[1152,3072]{1,0:T(8,128)(2,1)}, f32[24,3072]{1,0:T(8,128)}, f32[2...) custom-call(s32[2]{0:T(128)} %bitcast.15, ...), custom_call_target="tpu_custom_call" | custom-call | tf_op jit(solution)/shard_map/backward/pallas_call | solution.py:1275
  236.3 5.6 %finish.1 = (bf16[2,576,768]{2,1,0:T(8,128)(2,1)}, bf16[2,576,768]{2,1,0:T(8,128)(2,1)}, f32[24,2304]{1,0:T(8,128)}, f32[24,768]{1,0:T(8,128)}, f32[24,3072]{1,0...) custom-call(s32[8,576]{1,0:T(8,128)} %constant.7.clone.target, ...), custom_call_target="tpu_custom_call" | custom-call | tf_op jit(solution)/shard_map/finish/pallas_call | solution.py:1354

commit v2 on v1

--- a/solution.py
+++ b/solution.py
@@ -322,17 +322,23 @@
         self.send, self.recv = send, recv
         self.n = n_w + 3
 
-    def block(self, wide, p, c):
+    def block(self, wide, p, c, ab=None):
         if wide:
-            return (every, lanes(c * self.half + self.base + p * 256, 256))
-        return (every, lanes(c * (D // 2) + p * 128, 128))
-
-    def swap(self, wide, p, odd, s):
+            at, n = c * self.half + self.base + p * 256, 256
+            return (every, lanes(at, n) if ab is None else lanes(at + ab * 128, 128))
+        n = self.r.shape[3] // 2
+        return (every if ab is None else pl.ds(ab * n, n), lanes(c * (D // 2) + p * 128, 128))
+
+    def swaps(self, wide, p, s):
+        return [self.swap(wide, p, s, ab) for ab in ((None,) if s in (0, 3) else (0, 1))]
+
+    def swap(self, wide, p, s, ab):
         pc = self.place
         ref = self.w if wide else self.r
         q = p if wide else self.n_w + p
-        sems = (lambda k: self.send.at[q, s, k - 1], lambda k: self.recv.at[q, s, k - 1])
-        blk = self.block(wide, p, pc.c)
+        n = {0: 0, 1: 1, 2: 3, 3: 5}[s] + (ab or 0)
+        sems = (lambda k: self.send.at[q, n, k - 1], lambda k: self.recv.at[q, n, k - 1])
+        blk = self.block(wide, p, pc.c, ab)
         zs = every if wide else pl.ds(self.part * (pc.nz // 2), pc.nz // 2)
         at = lambda zz, yy, xx, b=blk: ref.at[(zz, yy, xx) + b]
         z, y, x = pc.z, pc.y, pc.x
@@ -343,7 +349,7 @@
         if s == 3:
             mine = lambda k: at(zs, every, every)
             return Swap(pc, "c", sems, mine, mine, lambda k: at(zs, every, every, self.block(wide, p, 1 - pc.c)))
-        first = "y" if odd else "x"
+        first = "xy"[ab]
         if s == 1:
             own = lambda k: at(zs, y, x)
             if first == "x":
@@ -359,17 +365,20 @@
         when(both(p >= 0, p < self.n_w), lambda: body(True, p))
         when(both(p >= self.n_w, p < self.n), lambda: body(False, p - self.n_w))
 
-    def tick(self, u, odd, landed=None):
+    def tick(self, u, landed=None):
         def last(wide, p):
-            self.swap(wide, p, odd, 3).arrive()
+            for swap in self.swaps(wide, p, 3):
+                swap.arrive()
             if landed is not None:
                 landed(wide, p)
 
         def step(s):
             def body(wide, p):
                 if s:
-                    self.swap(wide, p, odd, s - 1).arrive()
-                self.swap(wide, p, odd, s).start()
+                    for swap in self.swaps(wide, p, s - 1):
+                        swap.arrive()
+                for swap in self.swaps(wide, p, s):
+                    swap.start()
             return body
 
         self.on_piece(u - 8, last)
@@ -379,7 +388,8 @@
     def finish(self):
         for q in range(self.n):
             for s in range(4):
-                self.swap(q < self.n_w, q if q < self.n_w else q - self.n_w, q % 2 == 1, s).done()
+                for swap in self.swaps(q < self.n_w, q if q < self.n_w else q - self.n_w, s):
+                    swap.done()
 
 
 def small_swap(pc, sb, send, recv, s):
@@ -497,9 +507,9 @@
         for s in first[:-1]:
             s.arrive()
         w[pc.z, pc.y, pc.x, :, lanes(pc.c * HALF, HALF)] = stage_w[...].astype(BF16)
-        gather.tick(0, False)
+        gather.tick(0, landed)
         small_tick(0)
-        gather.tick(1, True)
+        gather.tick(1, landed)
         first[-1].arrive()
         r[pc.z, pc.y, pc.x, :, lanes(pc.c * (D // 2), D // 2)] = stage_r[...].astype(BF16)
         o_ew[...] = stage_w[:, TM_HALF + FF_PART:HALF].astype(BF16)
@@ -523,8 +533,7 @@
 
     def prologue(u, _):
         if near:
-            for odd in range(2):
-                pl.when(u % 2 == odd)(lambda odd=odd: gather.tick(u, odd == 1, landed))
+            gather.tick(u, landed)
             for k in range(1, 5):
                 pl.when(u == 2 * k)(lambda k=k: small_tick(2 * k))
 
@@ -600,8 +609,7 @@
         softmax(i + 1, g, 1)
         attend(i + 1, g, 1)
         if near:
-            for odd in range(2):
-                pl.when(q % 2 == odd)(lambda odd=odd: gather.tick(10 + q, odd == 1, landed))
+            gather.tick(10 + q, landed)
         return 0
 
     lax.fori_loop(0, 4 * GROUPS, quarter, 0)
@@ -658,7 +666,7 @@
                vm((ROWS, D), BF16), vm((ROWS, D), F32), vm((ROWS, D), BF16), vm((2, WT, QL), BF16),
                vm((HEADS, 4 * WT), F32), vm((GROUPS * 9, WT, 128), F32), vm((2, 16, QL), F32), vm((2, QL, GW), BF16),
                vm((2, WT, QL), F32), vm((2, WT, 128), jnp.int32), vm((4, WT, 128), jnp.int32), vm((4, WT, 128), jnp.int32),
-               dma((12, 4, peers)), dma((12, 4, peers)), dma((14, peers)), dma((14, peers)), dma((30,)), dma((2,))]
+               dma((12, 6, peers)), dma((12, 6, peers)), dma((14, peers)), dma((14, peers)), dma((30,)), dma((2,))]
     params = dict(collective_id=0, has_side_effects=True) if near else {}
     return pl.pallas_call(
         functools.partial(forward_kernel, near, dims),
@@ -808,7 +816,7 @@
 
 def backward_kernel(near, dims, counts, rasq, do, w, r, own_ew, own_er, triple_h, pt_h, att_h, mixed_h, n2_h, normed_h,
                     xp_h, sv, eb, o_out, o_dx, o_act, o_t, o_e, o_r, o_small, o_deb, o_t4,
-                    raster, ew, rw, dop, dn2, mixed, part, e0, e1, e2, e3, ef, t0, t1, t2, t3, tf, b0, b1, b2, b3, bf, slots_a, slots_g, late, slots_l, sums_g, smalls,
+                    raster, ew, rw, dop, dn2, mixed, part, e0, e1, e2, e3, ef, t0, t1, t2, t3, tf, b0, b1, b2, b3, bf, slots_a, slots_g, late, slots_l, smalls,
                     gsend, grecv, send, recv, ssend, srecv, lsem):
     def load(n, src, dst):
         return pltpu.make_async_copy(src, dst, lsem.at[n])
@@ -818,7 +826,7 @@
         rs = Scatter(pc, {"e": (e0, e1, e2, e3, ef), "t": (t0, t1, t2, t3, tf), "r": (b0, b1, b2, b3, bf)}, send, recv)
         sum_a = SmallSum(pc, slots_a, ssend.at[0], srecv.at[0])
         sum_l = SmallSum(pc, slots_l, ssend.at[1], srecv.at[1])
-        sum_g = lambda g: SmallSum(pc, slots_g.at[g], ssend.at[2 + g], srecv.at[2 + g])
+        sum_g = SmallSum(pc, slots_g, ssend.at[2], srecv.at[2])
         pc.greet()
     else:
         pc = None
@@ -849,8 +857,8 @@
             def _():
                 rw[pc.z, pc.y, pc.x, :, lanes(pc.c * (D // 2), D // 2)] = own_er[...]
 
-            gather.tick(0, False)
-            gather.tick(1, True)
+            gather.tick(0)
+            gather.tick(1)
 
         def permute(i, _):
             dop[window(i), :] = dot(to_window(raster, i % 4), do[i // 4]).astype(BF16)
@@ -858,8 +866,8 @@
 
         lax.fori_loop(0, 8, permute, 0)
         if near:
-            gather.tick(2, False)
-            gather.tick(3, True)
+            gather.tick(2)
+            gather.tick(3)
         for c in loads:
             c.wait()
         n2t[...] = n2[...].T
@@ -912,8 +920,8 @@
                 cc = lanes(n * 256, 256)
                 dn2[:, cc] += dot(hl[...], weights[n * 256:(n + 1) * 256], NT)
             if near:
-                gather.tick(4 + 2 * j, False)
-                gather.tick(5 + 2 * j, True)
+                gather.tick(4 + 2 * j)
+                gather.tick(5 + 2 * j)
                 for step in range(5, -1, -1):
                     i = j // 2 - step
                     pl.when(jnp.logical_and(lax.rem(j, 2) == 1, i >= 0))(
@@ -993,11 +1001,6 @@
                 dt[:, :, :, :, lanes(h * TM_HALF + lo, n)] = v[:, at:at + n].reshape(dt.shape[:4] + (n,))
                 at += n
 
-        def group_sum(g, m):
-            total = sum_g(g).advance(m)
-            if total is not None:
-                sums_g[g] = total
-
         def attention(datt, xt, xn, qs, dos, st, raw, pt, bgrad, accbuf, psem):
             loads = [load(0, att_h, xn), load(1, triple_h, triple), load(2, xp_h, xp)]
             loads += [load(4 + c, w.at[:, :, :, :, lanes(c * HALF, TM_HALF)], tw.at[:, :, :, :, lanes(c * TM_HALF, TM_HALF)])
@@ -1108,29 +1111,17 @@
                     for t in range(18, 24):
                         if events(t):
                             pl.when(q == t - 18)(lambda t=t: ert_tick(t))
-                    for m in range(4):
-                        k = (q - 2 - m) // 2
-
-                        def more(k=k, m=m):
-                            total = sum_g(2 - k).advance(m)
-                            if total is not None:
-                                sums_g[2 - k] = total
-
-                        pl.when(jnp.logical_and(q - 2 - m >= 0, lax.rem(q + 10 - m, 2) == 0))(more)
                     for m, at in enumerate((0, 2, 4)):
                         pl.when(q == at)(lambda m=m: sum_a.advance(m) and None)
 
-                    @pl.when(q % 2 == 1)
-                    def _():
-                        own = slots_g.at[g, pc.c]
-                        own[...] = jnp.zeros(own.shape, F32)
-                        own[0:8, 0:4 * WT] = t4g[pl.ds(aligned(g * GH, GH), GH), :]
-                        for k in range(2):
-                            own[8 + k:9 + k, 0:GW] = small[2 + k:3 + k, lanes(g * GW, GW)]
-                        sum_g(g).start()
                 return 0
 
             lax.fori_loop(0, 2 * GROUPS, half_group, 0)
+            if near:
+                own = slots_g.at[pc.c]
+                own[...] = jnp.zeros(own.shape, F32)
+                own[:, 0:4 * WT] = t4g[...]
+                sum_g.start()
         def rest(act):
             again = load(0, o_act, act)
             again.start()
@@ -1145,9 +1136,8 @@
                         @pl.when(n == t)
                         def _(t=t):
                             ert_tick(24 + t)
-                            group_sum(1, t + 2)
                             if t == 1:
-                                group_sum(0, 0)
+                                sum_g.advance(0)
                 return 0
 
             lax.fori_loop(0, 3, normed_grad, 0)
@@ -1164,10 +1154,11 @@
             late[...] = jnp.zeros(late.shape, F32)
             lax.fori_loop(0, 8, ln1b, 0)
             if near:
-                slots_l[pc.c] = late[0:2, :]
+                slots_l[pc.c, 0:2, :] = late[0:2, :]
+                slots_l[pc.c, 2:4, :] = small[2:4, :]
                 sum_l.start()
                 ert_tick(26)
-                group_sum(0, 1)
+                sum_g.advance(1)
                 sum_keep[...] = sum_a.advance(3)
             mixed_again = load(3, mixed_h, mixed)
             mixed_again.start()
@@ -1186,7 +1177,7 @@
                 c.start()
             if near:
                 ert_tick(27)
-                group_sum(0, 2)
+                sum_g.advance(2)
                 sum_l.advance(0)
             again.wait()
             mixed_again.wait()
@@ -1199,8 +1190,6 @@
                         @pl.when(n == t)
                         def _(t=t):
                             ert_tick(28 + t)
-                            if t == 0:
-                                group_sum(0, 3)
                             sum_l.advance(1 + t)
                 return 0
 
@@ -1211,26 +1200,24 @@
                 c.start()
             if near:
                 ert_tick(30)
+                total_g = sum_g.advance(3)
                 total_l = sum_l.advance(3)
                 dev = pc.z * (2 * pc.ny * pc.nx) + (pc.y * pc.nx + pc.x) * 2 + pc.c
                 n = o_small.shape[1]
                 shift = lax.rem(D - dev * n, D)
-                biases = [jnp.concatenate([sums_g[g, 8 + k:9 + k, 0:GW] for g in range(GROUPS)], axis=1) for k in range(2)]
-                rows = jnp.concatenate([total_l] + biases + [sum_keep[0:4, :]], axis=0)
+                rows = jnp.concatenate([total_l, sum_keep[0:4, :]], axis=0)
                 o_small[...] = pltpu.roll(rows, shift, axis=1)[:, 0:n]
                 wide_n = o_deb.shape[1]
                 per = D // wide_n
                 row = sum_keep[pl.ds(4 + dev // per, 1), :]
                 o_deb[...] = pltpu.roll(row, lax.rem(D - lax.rem(dev, per) * wide_n, D), axis=1)[:, 0:wide_n]
-                for g in range(GROUPS):
-                    o_t4[g * GH:(g + 1) * GH, :] = sums_g[g, 0:8, 0:4 * WT]
+                o_t4[...] = total_g[:, 0:4 * WT]
                 rs.done("e", None, o_e, 6, range(1, 5))
                 rs.done("r", None, o_r, 3, range(1, 5))
                 rs.done("t", dt, o_t, 6, range(5))
                 sum_a.done()
                 sum_l.done()
-                for g in range(GROUPS):
-                    sum_g(g).done()
+                sum_g.done()
             else:
                 o_small[0:2, :] = late[0:2]
                 o_small[2:8, :] = small[2:8, :]
@@ -1279,10 +1266,10 @@
         out_specs=[ANY] * 3 + ([VM] * 3 if near else [ANY] * 3) + [VM] * 3,
         scratch_shapes=[vm((4, WT, 128), jnp.int32), vm((nz, ny, nx, rw, FF), BF16), vm((nz, ny, nx, rr, D), BF16), vm((ROWS, D), BF16), vm((ROWS, D), F32),
                         vm((ROWS, D), F32), vm((ROWS, D), BF16)] + bufs
-        + [vm((n_slots, 8, D), F32), vm((GROUPS, n_slots, 16, 640), F32), vm((8, D), F32), vm((n_slots, 2, D), F32),
-           vm((GROUPS, 16, 640), F32), vm((16, D), F32),
-           dma((6, 4, peers)), dma((6, 4, peers)), dma((15, 2, 5, peers)), dma((15, 2, 5, peers)), dma((5, 4, peers)),
-           dma((5, 4, peers)), dma((7,))],
+        + [vm((n_slots, 8, D), F32), vm((n_slots, HEADS, 640), F32), vm((8, D), F32), vm((n_slots, 4, D), F32),
+           vm((16, D), F32),
+           dma((6, 6, peers)), dma((6, 6, peers)), dma((15, 2, 5, peers)), dma((15, 2, 5, peers)), dma((3, 4, peers)),
+           dma((3, 4, peers)), dma((7,))],
         name="backward",
         compiler_params=pltpu.CompilerParams(vmem_limit_bytes=VMEM_LIMIT, **params),
     )(counts, jnp.asarray(RASTER_Q), do, w, r, own_ew, own_er, triple, pt, att, mixed, n2, normed, xp, sv,

time: 242 us -> 229 us (0.946)
  Pallas kernels: 241 us -> 228 us
    pallas_call x1, Pallas kernels: 159 us -> 146 us  [backward(): pl.pallas_call(functools.partial(backward_kernel, near, dims), out_shape=...]
where the time goes in v2:
time: 229 us
  Pallas kernels  228 us (100%)
    pallas_call x1, Pallas kernels, backward(): pl.pallas_call(functools.partial(backward_kernel, near, dims), out_shape=...  146 us
    pallas_call x1, Pallas kernels, forward(): pl.pallas_call(functools.partial(forward_kernel, near, dims), out_shape=[...  76.1 us
    pallas_call x1, Pallas kernels, shards(): pl.pallas_call(finish_kernel, out_shape=[image, image] + [jax.ShapeDtypeS...  5.58 us

profile of v2, /device:TPU:0, one launch (start us, length us, event | category | flops | bytes accessed | tf_op | source)
XLA Modules:
  0.0 228.8 jit_solution(9603452814236208627)
XLA Ops:
  0.7 76.1 %forward.1 = (bf16[4,2,2,48,6144]{4,3,2,1,0:T(8,128)(2,1)}, bf16[4,2,2,192,768]{4,3,2,1,0:T(8,128)(2,1)}, bf16[1152,2304]{1,0:T(8,128)(2,1)}, bf16[24,144,1152]{...) custom-call(s32[2]{0:T(128)} %bitcast.14, ...), custom_call_target="tpu_custom_call" | custom-call | tf_op jit(solution)/shard_map/forward/pallas_call | solution.py:671
  76.8 146.2 %backward.1 = (bf16[2,576,768]{2,1,0:T(8,128)(2,1)}, bf16[2,576,768]{2,1,0:T(8,128)(2,1)}, bf16[1152,3072]{1,0:T(8,128)(2,1)}, f32[24,3072]{1,0:T(8,128)}, f32[2...) custom-call(s32[2]{0:T(128)} %bitcast.15, ...), custom_call_target="tpu_custom_call" | custom-call | tf_op jit(solution)/shard_map/backward/pallas_call | solution.py:1262
  223.0 5.6 %finish.1 = (bf16[2,576,768]{2,1,0:T(8,128)(2,1)}, bf16[2,576,768]{2,1,0:T(8,128)(2,1)}, f32[24,2304]{1,0:T(8,128)}, f32[24,768]{1,0:T(8,128)}, f32[24,3072]{1,0...) custom-call(s32[8,576]{1,0:T(8,128)} %constant.7.clone.target, ...), custom_call_target="tpu_custom_call" | custom-call | tf_op jit(solution)/shard_map/finish/pallas_call | solution.py:1341

commit v3 on v2

--- a/solution.py
+++ b/solution.py
@@ -300,6 +300,10 @@
         else:
             out = c if out is True else jnp.logical_and(out, c)
     return out
+
+
+def twos(n, body):
+    lax.fori_loop(0, n // 2, lambda i, _: (body(2 * i, 0), body(2 * i + 1, 0))[0], 0)
 
 
 def call(kernel, outs, scratch, ins, name):
@@ -504,12 +508,15 @@
         for n, src, dst, width in own_halves(pc.c):
             ref, stage = own[n], (stage_r if n == 3 else stage_w)
             stage[pl.ds(aligned(pc.c * ref.shape[0], 8), ref.shape[0]), lanes(dst, width)] = ref[:, lanes(src, width)]
-        for s in first[:-1]:
+        for s in first[:7]:
             s.arrive()
-        w[pc.z, pc.y, pc.x, :, lanes(pc.c * HALF, HALF)] = stage_w[...].astype(BF16)
+        w[pc.z, pc.y, pc.x, :, lanes(pc.c * HALF, TM_HALF)] = stage_w[:, 0:TM_HALF].astype(BF16)
         gather.tick(0, landed)
         small_tick(0)
         gather.tick(1, landed)
+        for s in first[7:9]:
+            s.arrive()
+        w[pc.z, pc.y, pc.x, :, lanes(pc.c * HALF + TM_HALF, FF_HALF)] = stage_w[:, TM_HALF:].astype(BF16)
         first[-1].arrive()
         r[pc.z, pc.y, pc.x, :, lanes(pc.c * (D // 2), D // 2)] = stage_r[...].astype(BF16)
         o_ew[...] = stage_w[:, TM_HALF + FF_PART:HALF].astype(BF16)
@@ -543,7 +550,8 @@
 
         @pl.when(jnp.logical_and(u >= 5, u < 9))
         def _():
-            lax.fori_loop(2 * (u - 5), 2 * (u - 4), permute, 0)
+            permute(2 * (u - 5), 0)
+            permute(2 * (u - 5) + 1, 0)
 
         return 0
 
@@ -556,7 +564,7 @@
         normed[window(i), :] = (hat * sv[0:1, :] + sv[1:2, :]).astype(BF16)
         return 0
 
-    lax.fori_loop(0, 8, ln1, 0)
+    twos(8, ln1)
     keep(24, xp, o_xp).start()
     keep(25, normed, o_normed).start()
     wf = Flat(w)
@@ -629,7 +637,7 @@
         n2[window(i), :] = (hat * sv[5:6, :] + sv[6:7, :]).astype(BF16)
         return 0
 
-    lax.fori_loop(0, 8, ln2, 0)
+    twos(8, ln2)
     keep(29, n2, o_n2).start()
     if near:
         gather.finish()
@@ -864,7 +872,7 @@
             dop[window(i), :] = dot(to_window(raster, i % 4), do[i // 4]).astype(BF16)
             return 0
 
-        lax.fori_loop(0, 8, permute, 0)
+        twos(8, permute)
         if near:
             gather.tick(2)
             gather.tick(3)
@@ -967,7 +975,7 @@
             part[rows, :] = m.astype(BF16)
             return 0
 
-        lax.fori_loop(0, 8, ln2b, 0)
+        twos(8, ln2b)
         if near:
             er_tick(15)
             gather.finish()
@@ -1152,7 +1160,7 @@
                 return 0
 
             late[...] = jnp.zeros(late.shape, F32)
-            lax.fori_loop(0, 8, ln1b, 0)
+            twos(8, ln1b)
             if near:
                 slots_l[pc.c, 0:2, :] = late[0:2, :]
                 slots_l[pc.c, 2:4, :] = small[2:4, :]
@@ -1169,7 +1177,7 @@
                     dst[window(k), :] = dot(to_raster(rasq, m), src[pl.ds(aligned(b * TOK, TOK), TOK), :]).astype(BF16)
                     return 0
 
-                lax.fori_loop(0, 8, block, 0)
+                twos(8, block)
 
             back_to_raster(ml, part)
             saves = [load(4 + b, part.at[b * TOK:(b + 1) * TOK, :], o_dx.at[b]) for b in range(2)]
@@ -1277,9 +1285,10 @@
 
 
 def finish_kernel(target, out_h, dx_h, t, e, r, small, deb, t4, out, dx, triple, merge, expand, reduce, table, *rest):
-    vectors = rest
-    out[...] = out_h[...]
-    dx[...] = dx_h[...]
+    vectors, sem = rest[:-1], rest[-1]
+    copies = [pltpu.make_async_copy(out_h, out, sem.at[0]), pltpu.make_async_copy(dx_h, dx, sem.at[1])]
+    for c in copies:
+        c.start()
     for g in range(GROUPS):
         for k, parts in enumerate(group_cols(g)):
             at = k * D + g * GW
@@ -1297,6 +1306,8 @@
     vectors[8][...] = deb[0, :]
     table[...] = lax.dot_general(t4[...], onehot(target), NT, precision=lax.Precision.HIGHEST,
                                  preferred_element_type=F32)
+    for c in copies:
+        c.wait()
 
 
 def weights_in_pieces(triple_weight, merge_weight, expand_weight):
@@ -1340,7 +1351,8 @@
     shapes = [(rows, 3 * D), (rows, D), (rows, FF), (rr, D), (HEADS, EXT * EXT)] + [(rows,)] * 8 + [(n,)]
     out, dx, tr, mg, ex, re, table, *vec = pl.pallas_call(
         finish_kernel, out_shape=[image, image] + [jax.ShapeDtypeStruct(s, F32) for s in shapes],
-        in_specs=[VM] * 9, out_specs=[VM] * (2 + len(shapes)), name="finish",
+        in_specs=[VM, ANY, ANY] + [VM] * 6, out_specs=[VM] * (2 + len(shapes)),
+        scratch_shapes=[pltpu.SemaphoreType.DMA((2,))], name="finish",
         compiler_params=pltpu.CompilerParams(vmem_limit_bytes=VMEM_LIMIT),
     )(jnp.asarray(TARGET), out, dx, gt, ge, gr, gs, gb, t4)
     return (out[:, None], dx[:, None], tr, mg, ex, re, *vec[:7], vec[8], vec[7], table.T)

time: 229 us -> 228 us (level)
  no operation moved by 1% of the time
where the time goes in v3:
time: 228 us; the launch traced here: 227 us
  Pallas kernels  227 us (100%)
    pallas_call x1, Pallas kernels, backward(): pl.pallas_call(functools.partial(backward_kernel, near, dims), out_shape=...  146 us
    pallas_call x1, Pallas kernels, forward(): pl.pallas_call(functools.partial(forward_kernel, near, dims), out_shape=[...  75.1 us
    pallas_call x1, Pallas kernels, shards(): pl.pallas_call(finish_kernel, out_shape=[image, image] + [jax.ShapeDtypeS...  5.32 us

profile of v3, /device:TPU:0, one launch (start us, length us, event | category | flops | bytes accessed | tf_op | source)
XLA Modules:
  0.0 227.5 jit_solution(10874713071604110991)
XLA Ops:
  0.7 75.1 %forward.1 = (bf16[4,2,2,48,6144]{4,3,2,1,0:T(8,128)(2,1)}, bf16[4,2,2,192,768]{4,3,2,1,0:T(8,128)(2,1)}, bf16[1152,2304]{1,0:T(8,128)(2,1)}, bf16[24,144,1152]{...) custom-call(s32[2]{0:T(128)} %bitcast.14, ...), custom_call_target="tpu_custom_call" | custom-call | tf_op jit(solution)/shard_map/forward/pallas_call | solution.py:679
  75.7 146.2 %backward.1 = (bf16[2,576,768]{2,1,0:T(8,128)(2,1)}, bf16[2,576,768]{2,1,0:T(8,128)(2,1)}, bf16[1152,3072]{1,0:T(8,128)(2,1)}, f32[24,3072]{1,0:T(8,128)}, f32[2...) custom-call(s32[2]{0:T(128)} %bitcast.15, ...), custom_call_target="tpu_custom_call" | custom-call | tf_op jit(solution)/shard_map/backward/pallas_call | solution.py:1270
  222.0 5.3 %finish.1 = (bf16[2,576,768]{2,1,0:T(8,128)(2,1)}, bf16[2,576,768]{2,1,0:T(8,128)(2,1)}, f32[24,2304]{1,0:T(8,128)}, f32[24,768]{1,0:T(8,128)}, f32[24,3072]{1,0...) custom-call(s32[8,576]{1,0:T(8,128)} %constant.7.clone.target, ...), custom_call_target="tpu_custom_call" | custom-call | tf_op jit(solution)/shard_map/finish/pallas_call | solution.py:1352
